TPU v7x, 256 devices: a whole 4x4x8 slice. The times are simulated.
256 devices in a mesh: band: 32 (over y_hi, z, core), fft: 8 (over y_lo, x).
Axes of the slice: x: 4, y: 4 (y_hi: 2, y_lo: 2; y = y_hi * 2 + y_lo), z: 8, core: 2. Of those that a mesh axis runs over, the one named last changes fastest.
Arguments:
- orbitals: float32 [64, 96, 9216], P('band', 'fft'), may hold values from -6 to 6
- owners: int32 [1], replicated, may hold values from 0 to 31
- cutoff_mask: int32 [96, 9216], P(None, 'fft'), may hold values from 0 to 1, as said below
Outputs:
- exchange_local: float32 [64, 96, 9216], P('band', 'fft')
- exchange_block: float32 [2, 96, 9216], P(None, 'fft')
Inputs may be any that keep to these rules, and one draw needn't show every extreme that they name: cutoff_mask is 1 exactly at the frequencies whose squared length s(x)^2 + s(y)^2 + s(z)^2 lies between 1 and a cutoff, and 0 elsewhere (0 at frequency (0, 0, 0)); it is unchanged when the sign of any one frequency component is changed.
All inputs are finite; a program needn't handle non-finite values.
Results may differ from a plain program's by a relative error of at most 0.00029.
Values sent between devices are 32-bit elements; how exact they have to be, the bound alone decides.
A program may use at most 128 MiB of HBM per device.

v0:
```python
import math

import jax
import jax.numpy as jnp
from jax import lax
from jax.sharding import PartitionSpec as P

COULOMB = 400.0
EXCHANGE_MIX = 0.25


def broadcast(value, axis, source):
    kept = jnp.where(lax.axis_index(axis) == source, value, 0).astype(value.dtype)
    return lax.psum(kept, axis)


def dft_tables(count):
    positions = jnp.arange(count, dtype=jnp.int32)
    phases = positions[:, None] * positions[None, :] % count
    angles = phases.astype(jnp.float32) * (2.0 * math.pi / count)
    return (jnp.cos(angles), jnp.sin(angles))


def transform_dim(values, matrix, dim):
    source = "pabc"
    target = source[:dim] + "k" + source[dim + 1 :]
    pattern = source + "," + source[dim] + "k" + "->" + target
    return jnp.einsum(pattern, values, matrix, precision=lax.Precision.HIGHEST)


def forward_local(real_data, cosine, sine):
    casine = cosine + sine
    parts = [transform_dim(transform_dim(real_data, casine, 3), casine, 2)]
    stacked = jnp.stack(parts, axis=1)
    return stacked.reshape(stacked.shape[0], stacked.shape[1], stacked.shape[2], -1)


def spectral_middle(spectrum, kernel, cosine, sine):
    count_pairs, components, grid_size, flat_cells = spectrum.shape
    shaped = spectrum.reshape(count_pairs, components, grid_size, kernel.shape[1], grid_size)
    casine = cosine + sine
    scaled = transform_dim(shaped[:, 0], casine, 1) * kernel
    parts = [transform_dim(scaled, casine, 1)]
    return jnp.stack(parts, axis=1).reshape(count_pairs, components, grid_size, flat_cells)


def inverse_local(spectrum, cosine, sine):
    count_pairs, components, slab_rows, flat_cells = spectrum.shape
    grid_size = cosine.shape[0]
    shaped = spectrum.reshape(count_pairs, components, slab_rows, grid_size, grid_size)
    casine = cosine + sine
    result = transform_dim(transform_dim(shaped[:, 0], casine, 2), casine, 3)
    result = result / float(grid_size * grid_size * grid_size)
    return result.reshape(count_pairs, slab_rows, flat_cells)


def per_device(orbitals, owners, cutoff_mask):
    local_bands, slab_rows, flat_cells = orbitals.shape
    grid_size = slab_rows * lax.axis_size("fft")
    cosine, sine = dft_tables(grid_size)
    positions = jnp.arange(grid_size, dtype=jnp.int32)
    signed = jnp.where(positions <= grid_size // 2, positions, positions - grid_size)
    signed_y = lax.dynamic_slice_in_dim(signed, lax.axis_index("fft") * slab_rows, slab_rows)
    squared = (
        signed[:, None, None] * signed[:, None, None]
        + signed_y[None, :, None] * signed_y[None, :, None]
        + signed[None, None, :] * signed[None, None, :]
    )
    weights = cutoff_mask.reshape(grid_size, slab_rows, grid_size).astype(jnp.float32)
    kernel = COULOMB * weights / jnp.maximum(squared, 1).astype(jnp.float32)
    local_total = jnp.zeros((local_bands, slab_rows, flat_cells), jnp.float32)
    block_orbs = broadcast(orbitals, "band", owners[0])
    pair_data = (orbitals[:, None] * block_orbs[None]).reshape(
        local_bands * local_bands, slab_rows, grid_size, grid_size
    )
    spectrum = forward_local(pair_data, cosine, sine)

    def one_pair(single):
        sent = lax.all_to_all(single[None], "fft", split_axis=3, concat_axis=2, tiled=True)
        pencil_out = spectral_middle(sent, kernel, cosine, sine)
        return lax.all_to_all(pencil_out, "fft", split_axis=2, concat_axis=3, tiled=True)[0]

    returned = lax.map(one_pair, spectrum)
    potential = inverse_local(returned, cosine, sine).reshape(
        local_bands, local_bands, slab_rows, flat_cells
    )
    local_total = local_total - EXCHANGE_MIX * jnp.sum(block_orbs[None] * potential, axis=1)
    block_terms = -EXCHANGE_MIX * jnp.sum(orbitals[:, None] * potential, axis=0)
    block_total = lax.psum(block_terms, "band")
    return (local_total, block_total)


def solution(mesh):
    in_specs = (P("band", "fft", None), P(), P(None, "fft"))
    out_specs = (P("band", "fft", None), P(None, "fft", None))
    return jax.shard_map(
        per_device, mesh=mesh, in_specs=in_specs, out_specs=out_specs, check_vma=False
    )
```

profile of v0, /device:TPU:1, one launch (start us, length us, event | category | flops | bytes accessed | tf_op | source)
XLA Modules:
  0.0 1006.4 jit_solution(8958187725105323984)
XLA Ops:
  7.9 1.3 broadcast_select_fusion
  10.0 267.7 %all-reduce.3.cloned.1.call-done = f32[2,12,9216]{2,0,1:T(2,128)} async-done(((f32[2,12,9216]{2,0,1:T(2,128)}), f32[2,12,9216]{2,0,1:T(2,128)}) %all-reduce.3.cloned.1.call-update) | async-done | bytes 884752 | tf_op jit(solution)/shard_map/psum | solution.py:14
  277.6 3.2 broadcast_multiply_fusion
  280.9 3.8 mul.147
  284.6 3.9 fusion.23
  288.6 3.8 convolution_bitcast_fusion.1
  292.4 12.8 %copy.59 = f32[4,12,96,96]{1,0,3,2:T(4,128)} copy(f32[4,12,96,96]{3,2,1,0:T(8,128)} %convolution_bitcast_fusion.1) | data formatting | bytes 3538944
  305.2 395.2 %while.14 = (s32[]{:T(128)}, f32[4,1,12,9216]{3,1,2,0:T(1,128)}, f32[4,1,12,9216]{2,1,0,3:T(1,128)}, f32[96,12,96]{0,2,1:T(8,128)S(1)}, s32[]{:T(128)}, /*index=5*/f32[]{:T(128)}, f32[]{:T(128)}) while((s32[]{:T(128)}, f32[4,1,12,9216]{3,1,2,0:T(1,128)}, f32[4,1,12,9216]{2,1,0,3:T(1,128)}, f32[96,12,96]{0,2,1:T(8,128)S(1)}, ...), condition=%wide.region_2.3_spmd.clone.clone, body=%wide.region_1.2_spmd.clone.clone.sunk | while | flops 255098880 | bytes 14155925 | solution.py:83
  317.5 4.9 fusion.62
  322.9 43.0 %reduce.5 = f32[9216,12]{1,0:T(8,128)} reduce(f32[9216,1,1,12]{3,2,1,0:T(1,128)} %fusion.62, f32[]{:T(128)} %broadcast.59), dimensions={1,2}, to_apply=%fusion.51.reduce_sub_computation | reduce | bytes 884740 | tf_op jit(solution)/shard_map/while
  365.9 6.0 reshape.105
  371.9 11.1 %all_to_all.58 = f32[8,1,13824]{2,1,0:T(1,128)S(1)} all-to-all(f32[8,1,13824]{2,1,0:T(1,128)S(1)} %reshape.105), channel_id=1, replica_groups=mesh['band'=32,'fft'=8] {'fft'}, dimensions={0} | all-to-all | bytes 884736 | tf_op jit(solution)/shard_map/while/body/eval_jaxpr/all_to_all | solution.py:79
  383.5 1.7 reduce.6
  385.2 10.4 %reshape.106 = f32[9216,1,1,12]{3,2,1,0:T(1,128)} reshape(f32[8,13824]{1,0:T(8,128)S(1)} %reduce.6) | data formatting | bytes 884736 | tf_op jit(solution)/shard_map/while
  395.6 3.4 copy.73
  399.5 1.3 convolution_multiply_fusion.2
  401.8 1.2 copy.75
  403.0 3.5 all-to-all-start.1
  406.5 7.0 all-to-all-done.1
  414.4 4.8 fusion.62
  419.8 43.0 %reduce.5 = f32[9216,12]{1,0:T(8,128)} reduce(f32[9216,1,1,12]{3,2,1,0:T(1,128)} %fusion.62, f32[]{:T(128)} %broadcast.59), dimensions={1,2}, to_apply=%fusion.51.reduce_sub_computation | reduce | bytes 884740 | tf_op jit(solution)/shard_map/while
  462.8 6.0 reshape.105
  468.8 9.6 all_to_all.58
  478.9 1.7 reduce.6
  480.6 10.4 %reshape.106 = f32[9216,1,1,12]{3,2,1,0:T(1,128)} reshape(f32[8,13824]{1,0:T(8,128)S(1)} %reduce.6) | data formatting | bytes 884736 | tf_op jit(solution)/shard_map/while
  491.0 3.4 copy.73
  494.9 1.3 convolution_multiply_fusion.2
  496.2 1.0 convolution_bitcast_fusion.3
  497.2 1.2 copy.75
  498.4 3.5 all-to-all-start.1
  501.9 7.0 all-to-all-done.1
  509.8 4.8 fusion.62
  515.2 43.0 %reduce.5 = f32[9216,12]{1,0:T(8,128)} reduce(f32[9216,1,1,12]{3,2,1,0:T(1,128)} %fusion.62, f32[]{:T(128)} %broadcast.59), dimensions={1,2}, to_apply=%fusion.51.reduce_sub_computation | reduce | bytes 884740 | tf_op jit(solution)/shard_map/while
  558.2 6.0 reshape.105
  564.2 9.5 all_to_all.58
  574.2 1.7 reduce.6
  575.9 10.4 %reshape.106 = f32[9216,1,1,12]{3,2,1,0:T(1,128)} reshape(f32[8,13824]{1,0:T(8,128)S(1)} %reduce.6) | data formatting | bytes 884736 | tf_op jit(solution)/shard_map/while
  586.3 3.4 copy.73
  590.2 1.3 convolution_multiply_fusion.2
  591.5 1.0 convolution_bitcast_fusion.3
  592.5 1.2 copy.75
  593.7 3.5 all-to-all-start.1
  597.2 7.0 all-to-all-done.1
  605.1 4.8 fusion.62
  610.5 43.0 %reduce.5 = f32[9216,12]{1,0:T(8,128)} reduce(f32[9216,1,1,12]{3,2,1,0:T(1,128)} %fusion.62, f32[]{:T(128)} %broadcast.59), dimensions={1,2}, to_apply=%fusion.51.reduce_sub_computation | reduce | bytes 884740 | tf_op jit(solution)/shard_map/while
  653.5 6.0 reshape.105
  659.5 9.5 all_to_all.58
  669.5 1.7 reduce.6
  671.2 10.4 %reshape.106 = f32[9216,1,1,12]{3,2,1,0:T(1,128)} reshape(f32[8,13824]{1,0:T(8,128)S(1)} %reduce.6) | data formatting | bytes 884736 | tf_op jit(solution)/shard_map/while
  681.6 3.4 copy.73
  685.5 1.3 convolution_multiply_fusion.2
  687.8 1.2 copy.75
  689.0 3.5 all-to-all-start.1
  692.5 7.0 all-to-all-done.1
  700.4 5.7 reduce
  706.1 2.0 reshape.97
  708.2 4.0 fusion.33
  712.2 2.2 fusion.25
  714.4 2.5 reshape.98
  716.9 8.7 multiply_reduce_fusion
  725.6 1.3 broadcast_multiply_fusion.1
  726.9 1.4 multiply_subtract_fusion
  728.3 268.7 %all-reduce.5.cloned.1.call-done = f32[2,12,9216]{2,0,1:T(2,128)} async-done(((f32[2,12,9216]{2,0,1:T(2,128)}), f32[2,12,9216]{2,0,1:T(2,128)}) %all-reduce.5.cloned.1.call-update) | async-done | bytes 884752 | tf_op jit(solution)/shard_map/psum | solution.py:89
  996.9 2.1 copy.89
  (42 shorter events, 12.3 us)
Async XLA Ops:
  7.2 2.1 copy-start.1
  7.2 270.5 %all-reduce.3.cloned.1.call-start = ((), (), s32[]{:S(2)}) async-start(), calls=%async_computation.2 | async-start | bytes 1769472 | tf_op jit(solution)/shard_map/psum | solution.py:14
  9.2 268.4 %copy-start = (f32[2,12,9216]{2,0,1:T(2,128)S(1)}, f32[2,12,9216]{2,0,1:T(2,128)}, u32[]{:S(2)}) copy-start(f32[2,12,9216]{2,0,1:T(2,128)} %param.5) | copy-start | bytes 2654212
  9.2 987.7 %all-reduce.5.cloned.1.call-start = ((), (), s32[]{:S(2)}) async-start(), calls=%async_computation.3 | async-start | bytes 1769472 | tf_op jit(solution)/shard_map/psum | solution.py:89
  403.0 10.5 %all-to-all-start.1 = ((f32[1,1,96,1152]{3,1,0,2:T(1,128)}), f32[1,1,96,1152]{3,1,0,2:T(1,128)S(1)}, u32[]{:S(2)}, u32[]{:S(2)}) async-start(f32[1,1,96,1152]{3,1,0,2:T(1,128)} %copy.75), calls=%async_computation.1 | async-start | bytes 884736 | tf_op jit(solution)/shard_map/while/body/eval_jaxpr/all_to_all | solution.py:81
  498.4 10.5 %all-to-all-start.1 = ((f32[1,1,96,1152]{3,1,0,2:T(1,128)}), f32[1,1,96,1152]{3,1,0,2:T(1,128)S(1)}, u32[]{:S(2)}, u32[]{:S(2)}) async-start(f32[1,1,96,1152]{3,1,0,2:T(1,128)} %copy.75), calls=%async_computation.1 | async-start | bytes 884736 | tf_op jit(solution)/shard_map/while/body/eval_jaxpr/all_to_all | solution.py:81
  593.7 10.5 %all-to-all-start.1 = ((f32[1,1,96,1152]{3,1,0,2:T(1,128)}), f32[1,1,96,1152]{3,1,0,2:T(1,128)S(1)}, u32[]{:S(2)}, u32[]{:S(2)}) async-start(f32[1,1,96,1152]{3,1,0,2:T(1,128)} %copy.75), calls=%async_computation.1 | async-start | bytes 884736 | tf_op jit(solution)/shard_map/while/body/eval_jaxpr/all_to_all | solution.py:81
  689.0 10.5 %all-to-all-start.1 = ((f32[1,1,96,1152]{3,1,0,2:T(1,128)}), f32[1,1,96,1152]{3,1,0,2:T(1,128)S(1)}, u32[]{:S(2)}, u32[]{:S(2)}) async-start(f32[1,1,96,1152]{3,1,0,2:T(1,128)} %copy.75), calls=%async_computation.1 | async-start | bytes 884736 | tf_op jit(solution)/shard_map/while/body/eval_jaxpr/all_to_all | solution.py:81
Sparse Core Ops, SparseCore 0:
  11.2 266.4 all-reduce.2
  727.0 269.8 all-reduce.4
where the time goes:
time: 1010 us
  waiting for transfers between devices  565 us (56%)
  other arithmetic  201 us (20%)
  local copies, waits for them, and re-layouts  136 us (13%)
  blocking collectives  39.7 us (4%)
  matrix products  23.2 us (2%)
  between operations  15.3 us (2%)
  starting transfers between devices  14 us (1%)
  loops' own time  12.6 us (1%)
    psum x1, waiting for transfers between devices, per_device(): block_total = lax.psum(block_terms, 'band')  269 us
    psum x1, waiting for transfers between devices, broadcast(): return lax.psum(kept, axis)  268 us
    while x4, other arithmetic  172 us
    while x16, local copies, waits for them, and re-layouts  86.9 us
    all_to_all x4, blocking collectives, one_pair(): lax.all_to_all(single[None], 'fft', split_axis=3, concat_axis=2, tiled=True)  39.7 us
    all_to_all x4, waiting for transfers between devices, one_pair(): lax.all_to_all(pencil_out, 'fft', split_axis=2, concat_axis=3, tiled=True)  28.1 us
    dot_general x12, matrix products, transform_dim(): return jnp.einsum(pattern, values, matrix, precision=lax.Precision.HIGHEST)  23.2 us
  transfers between devices with their start and end apart: 6, of which 6 were waited for; matrix products, arithmetic and copies ran while one was open for 0% of the time, Pallas kernels for 0%

commit v1 on v0

v1 whole, which is shorter than its diff:
```python
import functools
import math

import jax
import jax.numpy as jnp
import numpy as np
from jax import lax
from jax.experimental import pallas as pl
from jax.experimental.pallas import tpu as pltpu
from jax.sharding import PartitionSpec as P

COULOMB = 400.0
EXCHANGE_MIX = 0.25
NG = 96
NL = 2
NX = 12
NF = 8
NZ = 8
ROWS = NL * NX
LANES = NG * NG
CHUNK = NX * NG
QUADS = NG // 4
TILES = 27
PART = 14
MESH = pl.DeviceIdType.MESH
F32 = jnp.float32
BF16 = jnp.bfloat16


def split_const(matrix):
    high = matrix.astype(np.float32).astype(jnp.bfloat16)
    low = (matrix.astype(np.float64) - np.asarray(high, np.float64)).astype(jnp.bfloat16)
    return np.asarray(high), np.asarray(low)


def tables():
    index = np.arange(NG)
    angle = 2.0 * math.pi * (index[:, None] * index[None, :] % NG) / NG
    cas = np.cos(angle) + np.sin(angle)
    pack = np.zeros((4, 128, 4, NG))
    for b in range(4):
        pack[b, :NG, b, :] = cas
    pack = pack.reshape(512, 384)
    pack_h, pack_l = split_const(pack)
    open_h, open_l = split_const(pack.T)
    cas_h, cas_l = split_const(cas)
    zero = np.zeros_like(cas_h)
    left_y = np.concatenate(
        [np.concatenate([cas_h, cas_h], 1), np.concatenate([cas_l, zero], 1)], 0
    )
    both = np.zeros((NL, NG, NF, NL, NX))
    for i in range(NL):
        both[i, :, :, i, :] = cas.reshape(NG, NF, NX)
    both = both.reshape(NL * NG, NF * ROWS)
    fx_h, fx_l = split_const(both)
    bx_h, bx_l = split_const(both.T)
    left_fx = np.concatenate([fx_h, fx_l], 0)
    left_bx = np.concatenate([bx_h, bx_l], 0)
    return [pack_h, pack_l, open_h, open_l, left_y, left_fx, left_bx]


def dot(a, b):
    return lax.dot_general(a, b, (((1,), (0,)), ((), ())), preferred_element_type=F32)


def split(value):
    high = value.astype(BF16)
    low = (value - high.astype(F32)).astype(BF16)
    return high, low


def right_product(value, high, low):
    rows = value.shape[0]
    vh, vl = split(value)
    first = dot(jnp.concatenate([vh, vl], axis=0), high)
    return first[:rows] + first[rows:] + dot(vh, low)


def left_product(left, value):
    rows = left.shape[0] // 2
    vh, vl = split(value)
    first = dot(left, vh)
    return first[:rows] + first[rows:] + dot(left[:rows], vl)


def lane_iota():
    return lax.broadcasted_iota(jnp.int32, (ROWS, 128), 1)


def row_iota():
    return lax.broadcasted_iota(jnp.int32, (ROWS, 128), 0)


def open_quad(c0, c1, c2):
    lane = lane_iota()
    y1 = jnp.where(lane < 32, pltpu.roll(c0, 32, 1), pltpu.roll(c1, 32, 1))
    y2 = jnp.where(lane < 64, pltpu.roll(c1, 64, 1), pltpu.roll(c2, 64, 1))
    return c0, y1, y2, pltpu.roll(c2, 96, 1)


def close_quad(e0, e1, e2, e3):
    lane = lane_iota()
    r1 = pltpu.roll(e1, 96, 1)
    r2 = pltpu.roll(e2, 64, 1)
    r3 = pltpu.roll(e3, 32, 1)
    c0 = jnp.where(lane < 96, e0, r1)
    c1 = jnp.where(lane < 64, r1, r2)
    c2 = jnp.where(lane < 32, r2, r3)
    return c0, c1, c2


def rows_of(ref, lane):
    lane = pl.multiple_of(lane, 128)
    return jnp.concatenate(
        [ref[0, :, pl.ds(lane, 128)], ref[1, :, pl.ds(lane, 128)]], axis=0
    )


def plane_rows(y):
    return pl.ds(pl.multiple_of(y * ROWS, 8), ROWS)


def exchange_kernel(
    orb_ref, blk_ref, coulomb_ref, pack_h, pack_l, open_h, open_l, left_y, left_fx, left_bx,
    local_ref, block_ref,
    orb_u, dup, work, turned, block_u, local_u, send_a, recv_a, send_b, recv_b,
    ssem_a, rsem_a, ssem_b, rsem_b,
):
    me = lax.axis_index("fft")
    barrier = pltpu.get_barrier_semaphore()
    for o in range(1, NF):
        pl.semaphore_signal(
            barrier, inc=1, device_id={"fft": lax.rem(me + o, NF)}, device_id_type=MESH
        )

    def unpack(a, _):
        quad = open_quad(*[rows_of(orb_ref, a * 384 + 128 * k) for k in range(3)])
        for b in range(4):
            orb_u[plane_rows(4 * a + b), :] = quad[b]
        parts = [
            blk_ref[a // 3, pl.ds((a % 3) * 9 + 3 * k, 3)].reshape(ROWS, 128) for k in range(3)
        ]
        quad = open_quad(*parts)
        row = row_iota()
        for b in range(4):
            turn = pltpu.roll(quad[b], NX, 0)
            dup[0, plane_rows(4 * a + b), :] = jnp.where(row < NX, quad[b], turn)
            dup[1, plane_rows(4 * a + b), :] = jnp.where(row < NX, turn, quad[b])
        return 0

    lax.fori_loop(0, QUADS, unpack, 0)
    pl.semaphore_wait(barrier, NF - 1)

    def along_y(source, target):
        def step(k, _):
            pieces = [source[pl.ds(2 * k + s, NG, stride=ROWS), :] for s in range(2)]
            vh, vl = split(jnp.concatenate(pieces, axis=1))
            full = dot(left_y[...], jnp.concatenate([vh, vl], axis=0))
            out = full[:NG] + full[NG:]
            for s in range(2):
                target[pl.ds(2 * k + s, NG, stride=ROWS), :] = out[:, 128 * s : 128 * s + 128]
            return 0

        lax.fori_loop(0, ROWS // 2, step, 0)

    def copy_a(j, peer, slot):
        return pltpu.make_async_remote_copy(
            src_ref=send_a.at[j, peer],
            dst_ref=recv_a.at[j, slot],
            send_sem=ssem_a.at[j, peer],
            recv_sem=rsem_a.at[j, slot],
            device_id={"fft": peer},
            device_id_type=MESH,
        )

    def copy_b(j, peer, slot):
        return pltpu.make_async_remote_copy(
            src_ref=send_b.at[j, peer],
            dst_ref=recv_b.at[j, slot],
            send_sem=ssem_b.at[j, peer],
            recv_sem=rsem_b.at[j, slot],
            device_id={"fft": peer},
            device_id_type=MESH,
        )

    def packed(g):
        pieces = []
        for s in range(3):
            pieces.append(
                jnp.concatenate(
                    [turned[plane_rows(12 * g + 4 * s + b), :] for b in range(4)], axis=1
                )
            )
        return right_product(jnp.concatenate(pieces, axis=0), pack_h[...], pack_l[...])

    def forward(j):
        work[...] = orb_u[...] * dup[j]
        along_y(work, turned)

        def step(o, _):
            peer = lax.rem(me + o, NF)
            out = packed(peer)
            for s in range(3):
                send_a[j, peer, :, 384 * s : 384 * s + 384] = out[ROWS * s : ROWS * s + ROWS]
            copy_a(j, peer, me).start()
            return 0

        lax.fori_loop(1, NF, step, 0)
        out = packed(me)
        for s in range(3):
            recv_a[j, me, :, 384 * s : 384 * s + 384] = out[ROWS * s : ROWS * s + ROWS]

    def middle(j):
        for o in range(1, NF):
            peer = lax.rem(me + o, NF)
            copy_a(j, peer, peer).wait_recv()

        def step(s, _):
            cols = pl.ds(pl.multiple_of(384 * s, 128), 384)
            value = recv_a[j, :, :, cols].reshape(NF * ROWS, 384)
            spectrum = left_product(left_fx[...], value)
            weight = coulomb_ref[:, cols]
            scaled = jnp.concatenate([spectrum[:NG] * weight, spectrum[NG:] * weight], axis=0)
            back = left_product(left_bx[...], scaled)
            send_b[j, :, :, cols] = back.reshape(NF, ROWS, 384)
            return 0

        lax.fori_loop(0, 3, step, 0)
        recv_b[j, me] = send_b[j, me]
        for o in range(1, NF):
            copy_b(j, lax.rem(me + o, NF), me).start()

    def backward(j):
        for o in range(1, NF):
            peer = lax.rem(me + o, NF)
            copy_b(j, peer, peer).wait_recv()

        def step(g, _):
            value = jnp.concatenate(
                [recv_b[j, g, :, 384 * s : 384 * s + 384] for s in range(3)], axis=0
            )
            out = right_product(value, open_h[...], open_l[...])
            for s in range(3):
                for b in range(4):
                    turned[plane_rows(12 * g + 4 * s + b), :] = out[
                        ROWS * s : ROWS * s + ROWS, 128 * b : 128 * b + 128
                    ]
            return 0

        lax.fori_loop(0, NF, step, 0)
        along_y(turned, work)

        def finish(y, _):
            rows = plane_rows(y)
            pot = work[rows, :]
            term = dup[j, rows, :] * pot
            prod = orb_u[rows, :] * pot
            total = prod + pltpu.roll(prod, NX, 0)
            if j == 0:
                local_u[rows, :] = term
                block_u[rows, :] = total
            else:
                local_u[rows, :] = local_u[rows, :] + term
                block_u[rows, :] = jnp.where(row_iota() < NX, block_u[rows, :], total)
            return 0

        lax.fori_loop(0, NG, finish, 0)

    for j in range(NL):
        forward(j)
    for j in range(NL):
        middle(j)
    for j in range(NL):
        backward(j)

    def pack_out(a, _):
        local = close_quad(*[-EXCHANGE_MIX * local_u[plane_rows(4 * a + b), :] for b in range(4)])
        block = close_quad(*[-EXCHANGE_MIX * block_u[plane_rows(4 * a + b), :] for b in range(4)])
        for k in range(3):
            lanes = pl.ds(pl.multiple_of(a * 384 + 128 * k, 128), 128)
            local_ref[0, :, lanes] = local[k][:NX]
            local_ref[1, :, lanes] = local[k][NX:]
            block_ref[a // 3, pl.ds((a % 3) * 9 + 3 * k, 3)] = block[k].reshape(3, 8, 128)
        return 0

    lax.fori_loop(0, QUADS, pack_out, 0)
    for j in range(NL):
        for o in range(1, NF):
            peer = lax.rem(me + o, NF)
            copy_a(j, peer, me).wait_send()
            copy_b(j, peer, me).wait_send()


FAR = (4, 3, 5, 2, 6, 1, 7)


def sum_kernel(
    tiles_in, tiles_out, in_ref, out_ref,
    data, pair, part, gathered, summed, other, total, mate,
    ssem, rsem, zs_sem, zr_sem, gs_sem, gr_sem, ms_sem, mr_sem,
):
    band = lax.axis_index("band")
    core = lax.rem(band, 2)
    z = lax.rem(band // 2, NZ)
    yh = band // (2 * NZ)
    mate_core = 1 - core
    mate_band = band + 1 - 2 * core
    y_band = lax.rem(band + 2 * NZ, 4 * NZ)

    def z_band(other_z):
        return (yh * NZ + other_z) * 2 + core

    barrier = pltpu.get_barrier_semaphore()
    peers = [mate_band, y_band] + [z_band(lax.rem(z + o, NZ)) for o in range(1, NZ)]
    for peer in peers:
        pl.semaphore_signal(barrier, inc=1, device_id={"band": peer}, device_id_type=MESH)

    if tiles_in:
        source = in_ref
    else:
        source = data

        def load(c, _):
            value = rows_of(in_ref, c * 128)
            data[c // 9, pl.ds((c % 9) * 3, 3)] = value.reshape(3, 8, 128)
            return 0

        lax.fori_loop(0, 72, load, 0)
    pl.semaphore_wait(barrier, len(peers))

    def remote(src, dst, send, recv, peer):
        return pltpu.make_async_remote_copy(
            src_ref=src, dst_ref=dst, send_sem=send, recv_sem=recv,
            device_id={"band": peer}, device_id_type=MESH,
        )

    first = remote(
        source.at[:, pl.ds(13 * mate_core, PART)], pair, ssem.at[0], rsem.at[0], mate_band
    )
    first.start()
    first.wait_recv()

    def add_pair(k, _):
        part[k] = source[k, pl.ds(13 * core, PART)] + pair[k]
        return 0

    lax.fori_loop(0, NZ, add_pair, 0)

    def scatter(peer, slot):
        return remote(part.at[peer], gathered.at[slot], zs_sem.at[peer], zr_sem.at[slot], z_band(peer))

    for o in FAR:
        scatter(lax.rem(z + o, NZ), z).start()
    gathered[z] = part[z]
    for o in FAR:
        peer = lax.rem(z + o, NZ)
        scatter(peer, peer).wait_recv()
    value = gathered[0]
    for k in range(1, NZ):
        value = value + gathered[k]
    summed[...] = value
    second = remote(summed, other, ssem.at[1], rsem.at[1], y_band)
    second.start()
    second.wait_recv()
    total[z] = summed[...] + other[...]

    def spread(peer, slot):
        return remote(total.at[slot], total.at[slot], gs_sem.at[peer], gr_sem.at[slot], z_band(peer))

    def to_mate(slot):
        return remote(total.at[slot], mate.at[slot], ms_sem.at[slot], mr_sem.at[slot], mate_band)

    for o in FAR:
        spread(lax.rem(z + o, NZ), z).start()
    to_mate(z).start()
    for o in (1, 7, 2, 6, 3, 5, 4):
        peer = lax.rem(z + o, NZ)
        spread(peer, peer).wait_recv()
        to_mate(peer).start()
    for o in (0, 1, 7, 2, 6, 3, 5, 4):
        to_mate(lax.rem(z + o, NZ)).wait_recv()

    target = out_ref if tiles_out else data

    def merge(k, _):
        target[k, pl.ds(13 * core, PART)] = total[k]
        target[k, pl.ds(13 * mate_core, PART)] = mate[k]
        return 0

    first.wait_send()
    lax.fori_loop(0, NZ, merge, 0)
    if not tiles_out:

        def store(c, _):
            value = data[c // 9, pl.ds((c % 9) * 3, 3)].reshape(ROWS, 128)
            lanes = pl.ds(pl.multiple_of(c * 128, 128), 128)
            out_ref[0, :, lanes] = value[:NX]
            out_ref[1, :, lanes] = value[NX:]
            return 0

        lax.fori_loop(0, 72, store, 0)
    second.wait_send()
    for o in FAR:
        peer = lax.rem(z + o, NZ)
        scatter(peer, z).wait_send()
        spread(peer, z).wait_send()
    for o in range(NZ):
        to_mate(lax.rem(z + o, NZ)).wait_send()


TILE_SHAPE = (NZ, TILES, 8, 128)
FLAT_SHAPE = (NL, NX, LANES)


def all_sum(value, tiles_in, tiles_out, collective_id):
    vmem = pl.BlockSpec(memory_space=pltpu.VMEM)
    shape = TILE_SHAPE if tiles_out else FLAT_SHAPE
    piece = pltpu.VMEM((NZ, PART, 8, 128), F32)
    single = pltpu.VMEM((PART, 8, 128), F32)
    dma = pltpu.SemaphoreType.DMA
    return pl.pallas_call(
        functools.partial(sum_kernel, tiles_in, tiles_out),
        out_shape=jax.ShapeDtypeStruct(shape, F32),
        in_specs=[vmem],
        out_specs=vmem,
        scratch_shapes=[
            pltpu.VMEM(TILE_SHAPE, F32), piece, piece, piece, single, single, piece, piece,
            dma((2,)), dma((2,)), dma((NZ,)), dma((NZ,)), dma((NZ,)), dma((NZ,)),
            dma((NZ,)), dma((NZ,)),
        ],
        compiler_params=pltpu.CompilerParams(
            collective_id=collective_id, has_side_effects=True, vmem_limit_bytes=48 << 20
        ),
    )(value)


def exchange(orbitals, block, coulomb):
    vmem = pl.BlockSpec(memory_space=pltpu.VMEM)
    constants = [jnp.asarray(t) for t in tables()]
    plane = pltpu.VMEM((NG * ROWS, 128), F32)
    buffer = pltpu.VMEM((NL, NF, ROWS, CHUNK), F32)
    dma = pltpu.SemaphoreType.DMA
    return pl.pallas_call(
        exchange_kernel,
        out_shape=(
            jax.ShapeDtypeStruct(FLAT_SHAPE, F32),
            jax.ShapeDtypeStruct(TILE_SHAPE, F32),
        ),
        in_specs=[vmem] * 10,
        out_specs=(vmem, vmem),
        scratch_shapes=[
            plane, pltpu.VMEM((NL, NG * ROWS, 128), F32), plane, plane, plane, plane,
            buffer, buffer, buffer, buffer,
            dma((NL, NF)), dma((NL, NF)), dma((NL, NF)), dma((NL, NF)),
        ],
        compiler_params=pltpu.CompilerParams(
            collective_id=1, has_side_effects=True, vmem_limit_bytes=60 << 20
        ),
    )(orbitals, block, coulomb, *constants)


def coulomb_table(cutoff_mask):
    positions = jnp.arange(NG, dtype=jnp.int32)
    signed = jnp.where(positions <= NG // 2, positions, positions - NG)
    signed_y = lax.dynamic_slice_in_dim(signed, lax.axis_index("fft") * NX, NX)
    flat = jnp.repeat(signed_y * signed_y, NG) + jnp.tile(signed * signed, NX)
    squared = signed[:, None] * signed[:, None] + flat[None, :]
    weights = cutoff_mask.astype(F32)
    return COULOMB * weights / jnp.maximum(squared, 1).astype(F32) / float(NG**3)


def per_device(orbitals, owners, cutoff_mask):
    mine = lax.axis_index("band") == owners[0]
    kept = jnp.where(mine, orbitals, 0.0)
    block = all_sum(kept, False, True, 0)
    local, terms = exchange(orbitals, block, coulomb_table(cutoff_mask))
    return local, all_sum(terms, True, False, 2)


def solution(mesh):
    in_specs = (P("band", "fft", None), P(), P(None, "fft"))
    out_specs = (P("band", "fft", None), P(None, "fft", None))
    return jax.shard_map(
        per_device, mesh=mesh, in_specs=in_specs, out_specs=out_specs, check_vma=False
    )
```

time: 1010 us -> 148 us (0.15)
  waiting for transfers between devices: 565 us -> 0 us
  other arithmetic: 201 us -> 3.49 us
  Pallas kernels: 0 us -> 138 us
  local copies, waits for them, and re-layouts: 136 us -> 5.53 us
  blocking collectives: 39.7 us -> 0 us
  matrix products: 23.2 us -> 0 us
  starting transfers between devices: 14 us -> 0 us
  between operations: 15.3 us -> 1.43 us
  loops' own time: 12.6 us -> 0 us
    psum x2 -> x0, waiting for transfers between devices: 536 us -> none  [the longest x1 269 us: per_device(): block_total = lax.psum(block_terms, 'band')]
    while x5 -> x0, other arithmetic: 178 us -> none
    pallas_call x0 -> x3, Pallas kernels: none -> 138 us  [the longest x2 75.7 us: all_sum(): pl.pallas_call(functools.partial(sum_kernel, tiles_in, tiles_out), out_sh...]
    while x16 -> x0, local copies, waits for them, and re-layouts: 86.9 us -> none
    all_to_all x4 -> x0, blocking collectives: 39.7 us -> none  [one_pair(): lax.all_to_all(single[None], 'fft', split_axis=3, concat_axis=2, tiled=True)]
    all_to_all x4 -> x0, waiting for transfers between devices: 28.1 us -> none  [one_pair(): lax.all_to_all(pencil_out, 'fft', split_axis=2, concat_axis=3, tiled=True)]
    dot_general x12 -> x0, matrix products: 23.2 us -> none  [transform_dim(): return jnp.einsum(pattern, values, matrix, precision=lax.Precision.HIGHEST)]
    all_to_all x16 -> x0, local copies, waits for them, and re-layouts: 16.1 us -> none  [the longest x12 15.9 us: one_pair(): lax.all_to_all(single[None], 'fft', split_axis=3, concat_axis=2, tiled=True)]
  transfers between devices with their start and end apart: 6 -> 0, of which waited for: 6 -> 0; matrix products, arithmetic and copies ran while one was open for 0% -> 0% of each run, Pallas kernels for 0% -> 0%
where the time goes in v1:
time: 148 us
  Pallas kernels  138 us (93%)
  local copies, waits for them, and re-layouts  5.53 us (4%)
  other arithmetic  3.49 us (2%)
    pallas_call x2, Pallas kernels, all_sum(): pl.pallas_call(functools.partial(sum_kernel, tiles_in, tiles_out), out_sh...  75.7 us
    pallas_call x1, Pallas kernels, exchange(): pl.pallas_call(exchange_kernel, out_shape=(jax.ShapeDtypeStruct(FLAT_SHAP...  62.1 us
    unnamed x8, local copies, waits for them, and re-layouts  5.45 us

profile of v1, /device:TPU:1, one launch (start us, length us, event | category | flops | bytes accessed | tf_op | source)
XLA Modules:
  0.0 148.3 jit_solution(16178589510648767121)
XLA Ops:
  0.6 0.0 copy-start.2
  1.4 0.1 dynamic-slice_multiply_fusion
  1.5 0.1 broadcast_add_fusion
  1.5 0.1 add.38
  1.6 2.0 %divide_multiply_fusion.coulomb_ref = f32[96,1152]{1,0:T(8,128)} fusion(s32[96,1152]{1,0:T(8,128)} %param.12, s32[1152]{0:T(1024)S(1)} %add.38, s32[96]{0:T(128)S(1)} %fusion), kind=kLoop, calls=%fused_computation.1 | loop fusion | flops 774144 | bytes 889728 | tf_op jit(solution)/shard_map/div | solution.py:469
  3.6 0.0 copy-done.2
  3.6 1.4 broadcast_select_fusion
  5.0 41.1 %shard_map.113.blk_ref = f32[8,27,8,128]{3,2,1,0:T(8,128)S(1)} custom-call(f32[2,12,9216]{2,1,0:T(8,128)S(1)} %get-tuple-element.8.in_ref), custom_call_target="tpu_custom_call" | custom-call | tf_op jit(solution)/shard_map/pallas_call | solution.py:421
  46.1 0.0 copy-start
  46.1 0.9 copy-done
  47.0 62.1 %shard_map.114 = (f32[2,12,9216]{2,1,0:T(8,128)}, f32[8,27,8,128]{3,2,1,0:T(8,128)}) custom-call(f32[2,12,9216]{2,1,0:T(8,128)} %get-tuple-element.9.orb_ref, f32[8,27,8,128]{3,2,1,0:T(8,128)} %copy-done, f32[96,1152]{1,0:T(8,128)} %divide_multiply_fusion.coulomb_ref, bf16[512,384]{1,0:T(8,128)(2,1)} %constant.43.clone.pack_h, ...), custom_call_target="tpu_custom_call" | custom-call | tf_op jit(solution)/shard_map/pallas_call | solution.py:443
  109.1 0.0 copy-start.1
  109.1 2.9 %copy.14 = f32[2,12,9216]{2,0,1:T(2,128)} copy(f32[2,12,9216]{2,1,0:T(8,128)} %get-tuple-element.6) | data formatting | bytes 1769472
  112.1 0.0 copy-done.1
  112.1 34.6 %shard_map.115 = f32[2,12,9216]{2,1,0:T(8,128)S(1)} custom-call(f32[8,27,8,128]{3,2,1,0:T(8,128)S(1)} %copy-done.1), custom_call_target="tpu_custom_call" | custom-call | tf_op jit(solution)/shard_map/pallas_call | solution.py:421
  146.7 1.6 %copy.15 = f32[2,12,9216]{2,0,1:T(2,128)} copy(f32[2,12,9216]{2,1,0:T(8,128)S(1)} %shard_map.115) | data formatting | bytes 1769472
  (2 shorter events, 0.0 us)
Async XLA Ops:
  0.6 3.0 %copy-start.2 = (f32[2,12,9216]{2,0,1:T(2,128)S(1)}, f32[2,12,9216]{2,0,1:T(2,128)}, u32[]{:S(2)}) copy-start(f32[2,12,9216]{2,0,1:T(2,128)} %param.10) | copy-start | bytes 2654212
  46.1 0.9 copy-start
  109.1 3.0 %copy-start.1 = (f32[8,27,8,128]{3,2,1,0:T(8,128)S(1)}, f32[8,27,8,128]{3,2,1,0:T(8,128)}, u32[]{:S(2)}) copy-start(f32[8,27,8,128]{3,2,1,0:T(8,128)} %get-tuple-element.5.in_ref) | copy-start | bytes 2654212

commit v2 on v0

v2 whole, which is shorter than its diff:
```python
import math

import jax
import jax.numpy as jnp
import numpy as np
from jax import lax
from jax.experimental import pallas as pl
from jax.experimental.pallas import tpu as pltpu
from jax.sharding import PartitionSpec as P

COULOMB = 400.0
EXCHANGE_MIX = 0.25
NG = 96
NL = 2
NX = 12
NF = 8
NZ = 8
NT = 3
LANES = NG * NG
CHUNK = NX * NG
QUADS = NG // 4
PLANES = NG * 8
PART = 5
MESH = pl.DeviceIdType.MESH
F32 = jnp.float32
BF16 = jnp.bfloat16
FAR = (4, 3, 5, 2, 6, 1, 7)
NEAR = (1, 7, 2, 6, 3, 5, 4)


def split_const(matrix):
    high = matrix.astype(np.float32).astype(jnp.bfloat16)
    low = (matrix.astype(np.float64) - np.asarray(high, np.float64)).astype(jnp.bfloat16)
    return np.asarray(high), np.asarray(low)


def tables():
    index = np.arange(NG)
    angle = 2.0 * math.pi * (index[:, None] * index[None, :] % NG) / NG
    cas = np.cos(angle) + np.sin(angle)
    cas_h, cas_l = split_const(cas)
    zero = np.zeros_like(cas_h)
    left_y = np.concatenate(
        [np.concatenate([cas_h, cas_h], 1), np.concatenate([cas_l, zero], 1)], 0
    )
    right_z = np.zeros((256, 256), cas_h.dtype)
    right_z[:NG, :NG] = cas_h
    right_z[128 : 128 + NG, :NG] = cas_h
    right_z[:NG, 128 : 128 + NG] = cas_l
    both = np.zeros((NL, NG, NT, NF, NL, 4))
    for i in range(NL):
        both[i, :, :, :, i, :] = cas.reshape(NG, NF, NT, 4).transpose(0, 2, 1, 3)
    both = both.reshape(NL * NG, NL * NG)
    left_fx = np.concatenate(split_const(both), 0)
    left_bx = np.concatenate(split_const(both.T), 0)
    signed = np.where(index <= NG // 2, index, index - NG)
    lane_y = np.tile(np.repeat(np.arange(NX), NG)[None], (8, 1)).astype(np.int32)
    lane_z = np.tile(np.tile(signed * signed, NX)[None], (8, 1)).astype(np.int32)
    row_x = np.tile((signed * signed)[:, None], (1, 128)).astype(np.int32)
    return [left_y, right_z, left_fx, left_bx, lane_y, lane_z, row_x]


def dot(a, b):
    return lax.dot_general(a, b, (((1,), (0,)), ((), ())), preferred_element_type=F32)


def split(value):
    high = value.astype(BF16)
    low = (value - high.astype(F32)).astype(BF16)
    return high, low


def left_product(left, value):
    rows = left.shape[0] // 2
    vh, vl = split(value)
    first = dot(left, vh)
    return first[:rows] + first[rows:] + dot(left[:rows], vl)


def open_quad(c0, c1, c2):
    lane = lax.broadcasted_iota(jnp.int32, (8, 128), 1)
    y1 = jnp.where(lane < 32, pltpu.roll(c0, 32, 1), pltpu.roll(c1, 32, 1))
    y2 = jnp.where(lane < 64, pltpu.roll(c1, 64, 1), pltpu.roll(c2, 64, 1))
    return c0, y1, y2, pltpu.roll(c2, 96, 1)


def close_quad(e0, e1, e2, e3):
    lane = lax.broadcasted_iota(jnp.int32, (8, 128), 1)
    r1 = pltpu.roll(e1, 96, 1)
    r2 = pltpu.roll(e2, 64, 1)
    r3 = pltpu.roll(e3, 32, 1)
    c0 = jnp.where(lane < 96, e0, r1)
    c1 = jnp.where(lane < 64, r1, r2)
    c2 = jnp.where(lane < 32, r2, r3)
    return c0, c1, c2


def plane(y):
    return pl.ds(pl.multiple_of(y * 8, 8), 8)


def across(row):
    return pl.ds(row, NG, stride=8)


def kernel(
    orb_ref, keep_ref, mask_ref, left_y, right_z, left_fx, left_bx, lane_y, lane_z, row_x,
    local_ref, block_ref,
    coulomb, orb_t, source, full, orb_u, blk_u, turned, local_u, block_u,
    send_a, recv_a, send_b, recv_b, pair, part, gathered, summed, other, total, mate,
    sa_sem, ra_sem, sb_sem, rb_sem, ps_sem, pr_sem, ys_sem, yr_sem,
    zs_sem, zr_sem, gs_sem, gr_sem, ms_sem, mr_sem,
):
    me = lax.axis_index("fft")
    band = lax.axis_index("band")
    core = lax.rem(band, 2)
    z = lax.rem(band // 2, NZ)
    yh = band // (2 * NZ)
    mate_band = band + 1 - 2 * core
    y_band = lax.rem(band + 2 * NZ, 4 * NZ)

    def z_band(other_z):
        return (yh * NZ + other_z) * 2 + core

    def turn(o):
        return lax.rem(me + o, NF)

    def turn_z(o):
        return lax.rem(z + o, NZ)

    barrier = pltpu.get_barrier_semaphore()
    devices = [{"fft": turn(o)} for o in range(1, NF)]
    devices += [{"band": mate_band}, {"band": y_band}]
    devices += [{"band": z_band(turn_z(o))} for o in range(1, NZ)]
    for device in devices:
        pl.semaphore_signal(barrier, inc=1, device_id=device, device_id_type=MESH)

    def remote(src, dst, send, recv, device):
        return pltpu.make_async_remote_copy(
            src_ref=src, dst_ref=dst, send_sem=send, recv_sem=recv,
            device_id=device, device_id_type=MESH,
        )

    def copy_a(j, t, peer, slot):
        return remote(
            send_a.at[j, t, peer], recv_a.at[j, t, slot],
            sa_sem.at[j, t, peer], ra_sem.at[j, t, slot], {"fft": peer},
        )

    def copy_b(j, t, peer, slot):
        return remote(
            send_b.at[j, t, peer], recv_b.at[j, t, slot],
            sb_sem.at[j, t, peer], rb_sem.at[j, t, slot], {"fft": peer},
        )

    def to_pair(q, t):
        return remote(
            source.at[q, t, :, pl.ds(4 * (1 - core), PART)], pair.at[q, t],
            ps_sem.at[q, t], pr_sem.at[q, t], {"band": mate_band},
        )

    def scatter(q, t, peer, slot):
        return remote(
            part.at[q, t, peer], gathered.at[q, t, slot],
            zs_sem.at[q, t, peer], zr_sem.at[q, t, slot], {"band": z_band(peer)},
        )

    def to_y(q, t):
        return remote(
            summed.at[q, t], other.at[q, t], ys_sem.at[q, t], yr_sem.at[q, t], {"band": y_band}
        )

    def spread(q, t, peer, slot):
        return remote(
            total.at[q, t, slot], total.at[q, t, slot],
            gs_sem.at[q, t, peer], gr_sem.at[q, t, slot], {"band": z_band(peer)},
        )

    def to_mate(q, t, slot):
        return remote(
            total.at[q, t, slot], mate.at[q, t, slot],
            ms_sem.at[q, t, slot], mr_sem.at[q, t, slot], {"band": mate_band},
        )

    def sum_a(q, t):
        to_pair(q, t).start()

    def sum_b(q, t):
        to_pair(q, t).wait_recv()

        def step(k, _):
            part[q, t, k] = source[q, t, k, pl.ds(4 * core, PART)] + pair[q, t, k]
            return 0

        lax.fori_loop(0, NZ, step, 0, unroll=2)
        for o in FAR:
            scatter(q, t, turn_z(o), z).start()
        gathered[q, t, z] = part[q, t, z]

    def sum_c(q, t):
        for o in FAR:
            scatter(q, t, turn_z(o), turn_z(o)).wait_recv()
        value = gathered[q, t, 0]
        for k in range(1, NZ):
            value = value + gathered[q, t, k]
        summed[q, t] = value
        to_y(q, t).start()

    def sum_d(q, t):
        to_y(q, t).wait_recv()
        total[q, t, z] = summed[q, t] + other[q, t]
        for o in FAR:
            spread(q, t, turn_z(o), z).start()
        to_mate(q, t, z).start()

    def sum_e(q, t):
        for o in NEAR:
            spread(q, t, turn_z(o), turn_z(o)).wait_recv()
            to_mate(q, t, turn_z(o)).start()

    def sum_f(q, t):
        for o in (0,) + NEAR:
            to_mate(q, t, turn_z(o)).wait_recv()

        def step(k, _):
            full[q, t, k, pl.ds(4 * core, PART)] = total[q, t, k]
            full[q, t, k, pl.ds(4 * (1 - core), PART)] = mate[q, t, k]
            return 0

        lax.fori_loop(0, NZ, step, 0, unroll=2)

    def load_tiles(c, _):
        lanes = pl.ds(pl.multiple_of(c * 128, 128), 128)
        rows0, rows1 = orb_ref[0, :, lanes], orb_ref[1, :, lanes]
        keep = keep_ref[...]
        for t in range(NT):
            tile = jnp.concatenate([rows0[4 * t : 4 * t + 4], rows1[4 * t : 4 * t + 4]], axis=0)
            orb_t[t, c // 9, c % 9] = tile
            source[0, t, c // 9, c % 9] = tile * keep
        return 0

    lax.fori_loop(0, LANES // 128, load_tiles, 0, unroll=4)
    pl.semaphore_wait(barrier, len(devices))
    for t in range(NT):
        sum_a(0, t)

    low = lax.rem(me, NF) * NX + lane_y[...]
    low = jnp.where(low <= NG // 2, low, low - NG)
    flat = low * low + lane_z[...]

    def coulomb_rows(k, _):
        rows = pl.ds(pl.multiple_of(8 * k, 8), 8)
        squared = jnp.concatenate([row_x[rows, :]] * 9, axis=1) + flat
        weight = mask_ref[rows, :].astype(F32)
        scale = -EXCHANGE_MIX * COULOMB / float(NG**3)
        coulomb[rows, :] = scale * weight / jnp.maximum(squared, 1).astype(F32)
        return 0

    lax.fori_loop(0, NG // 8, coulomb_rows, 0)
    for t in range(NT):
        sum_b(0, t)

    def open_orb(a, _):
        for t in range(NT):
            quad = open_quad(*[orb_t[t, a // 3, (a % 3) * 3 + k] for k in range(3)])
            for b in range(4):
                orb_u[t, plane(4 * a + b), :] = quad[b]
        return 0

    lax.fori_loop(0, QUADS, open_orb, 0, unroll=2)
    for t in range(NT):
        sum_c(0, t)
    for t in range(NT):
        sum_d(0, t)

    def open_blk(t):
        def step(a, _):
            quad = open_quad(*[full[0, t, a // 3, (a % 3) * 3 + k] for k in range(3)])
            for b in range(4):
                blk_u[t, plane(4 * a + b), :] = quad[b]
            return 0

        lax.fori_loop(0, QUADS, step, 0, unroll=4)

    def transform_y(p0, p1):
        vh, vl = split(jnp.concatenate([p0, p1], axis=1))
        out = dot(left_y[...], jnp.concatenate([vh, vl], axis=0))
        out = out[:NG] + out[NG:]
        return out[:, :128], out[:, 128:]

    def transform_z(value):
        vh, vl = split(value)
        out = dot(jnp.concatenate([vh, vl], axis=1), right_z[...])
        return out[:, :128] + out[:, 128:]

    def forward(j, t):
        def rows(s, _):
            blk = blk_u[t, across(4 * j + s), :]
            out0, out1 = transform_y(
                orb_u[t, across(s), :] * blk, orb_u[t, across(4 + s), :] * blk
            )
            turned[across(s), :] = out0
            turned[across(4 + s), :] = out1
            return 0

        lax.fori_loop(0, 4, rows, 0, unroll=2)

        def half(h, _):
            out = transform_z(turned[pl.ds(pl.multiple_of(384 * h, 8), 384), :])
            for g in range(4):
                for s in range(3):
                    base = 96 * g + 32 * s
                    tiles = close_quad(*[out[base + 8 * b : base + 8 * b + 8] for b in range(4)])
                    for k in range(3):
                        lane = 384 * s + 128 * k
                        send_a[j, t, 4 * h + g, :, lane : lane + 128] = tiles[k]
            return 0

        lax.fori_loop(0, 2, half, 0)
        for o in range(1, NF):
            copy_a(j, t, turn(o), me).start()
        recv_a[j, t, me] = send_a[j, t, me]

    def middle(j):
        for t in range(NT):
            for o in range(1, NF):
                copy_a(j, t, turn(o), turn(o)).wait_recv()

        def step(s, _):
            cols = pl.ds(pl.multiple_of(384 * s, 128), 384)
            value = recv_a[j, :, :, :, cols].reshape(NL * NG, 384)
            spectrum = left_product(left_fx[...], value)
            weight = coulomb[:, cols]
            scaled = jnp.concatenate([spectrum[:NG] * weight, spectrum[NG:] * weight], axis=0)
            back = left_product(left_bx[...], scaled)
            send_b[j, :, :, :, cols] = back.reshape(NT, NF, 8, 384)
            return 0

        lax.fori_loop(0, 3, step, 0)
        for t in range(NT):
            for o in range(1, NF):
                copy_b(j, t, turn(o), me).start()
            recv_b[j, t, me] = send_b[j, t, me]

    def backward(j, t):
        for o in range(1, NF):
            copy_b(j, t, turn(o), turn(o)).wait_recv()

        def half(h, _):
            planes = []
            for g in range(4):
                for s in range(3):
                    planes += open_quad(
                        *[
                            recv_b[j, t, 4 * h + g, :, 384 * s + 128 * k : 384 * s + 128 * k + 128]
                            for k in range(3)
                        ]
                    )
            out = transform_z(jnp.concatenate(planes, axis=0))
            turned[pl.ds(pl.multiple_of(384 * h, 8), 384), :] = out
            return 0

        lax.fori_loop(0, 2, half, 0)

        def rows(s, _):
            pot0, pot1 = transform_y(turned[across(s), :], turned[across(4 + s), :])
            blk = blk_u[t, across(4 * j + s), :]
            term0, term1 = blk * pot0, blk * pot1
            if j > 0:
                term0 = local_u[t, across(s), :] + term0
                term1 = local_u[t, across(4 + s), :] + term1
            local_u[t, across(s), :] = term0
            local_u[t, across(4 + s), :] = term1
            block_u[t, across(4 * j + s), :] = (
                orb_u[t, across(s), :] * pot0 + orb_u[t, across(4 + s), :] * pot1
            )
            return 0

        lax.fori_loop(0, 4, rows, 0, unroll=2)

    def close_block(t):
        def step(a, _):
            tiles = close_quad(*[block_u[t, plane(4 * a + b), :] for b in range(4)])
            for k in range(3):
                source[1, t, a // 3, (a % 3) * 3 + k] = tiles[k]
            return 0

        lax.fori_loop(0, QUADS, step, 0, unroll=4)

    def write(ref, t, column, tile):
        lanes = pl.ds(pl.multiple_of(column * 128, 128), 128)
        ref[0, 4 * t : 4 * t + 4, lanes] = tile[:4]
        ref[1, 4 * t : 4 * t + 4, lanes] = tile[4:]

    def write_local(a, _):
        for t in range(NT):
            tiles = close_quad(*[local_u[t, plane(4 * a + b), :] for b in range(4)])
            for k in range(3):
                write(local_ref, t, 3 * a + k, tiles[k])
        return 0

    def write_block(t):
        def step(c, _):
            write(block_ref, t, c, full[1, t, c // 9, c % 9])
            return 0

        lax.fori_loop(0, LANES // 128, step, 0, unroll=4)

    for t in range(NT):
        sum_e(0, t)
        sum_f(0, t)
        open_blk(t)
        forward(0, t)
    for t in range(NT):
        forward(1, t)
    middle(0)
    middle(1)
    for t in range(NT):
        backward(0, t)
    backward(1, 0)
    close_block(0)
    sum_a(1, 0)
    backward(1, 1)
    close_block(1)
    sum_a(1, 1)
    sum_b(1, 0)
    backward(1, 2)
    close_block(2)
    sum_a(1, 2)
    sum_b(1, 1)
    sum_c(1, 0)
    sum_b(1, 2)
    lax.fori_loop(0, QUADS, write_local, 0, unroll=2)
    sum_d(1, 0)
    sum_c(1, 1)
    sum_d(1, 1)
    sum_c(1, 2)
    sum_d(1, 2)
    for t in range(NT):
        sum_e(1, t)
    for t in range(NT):
        sum_f(1, t)
        write_block(t)
    for t in range(NT):
        for j in range(NL):
            for o in range(1, NF):
                copy_a(j, t, turn(o), me).wait_send()
                copy_b(j, t, turn(o), me).wait_send()
            to_pair(j, t).wait_send()
            to_y(j, t).wait_send()
            to_mate(j, t, z).wait_send()
            for o in range(1, NZ):
                scatter(j, t, turn_z(o), z).wait_send()
                spread(j, t, turn_z(o), z).wait_send()
                to_mate(j, t, turn_z(o)).wait_send()


def per_device(orbitals, owners, cutoff_mask):
    mine = lax.axis_index("band") == owners[0]
    keep = jnp.broadcast_to(mine.astype(F32), (8, 128))
    vmem = pl.BlockSpec(memory_space=pltpu.VMEM)
    dma = pltpu.SemaphoreType.DMA

    def buffer(*shape):
        return pltpu.VMEM(shape, F32)

    planes = buffer(NT, PLANES, 128)
    tiles = buffer(2, NT, NZ, 9, 8, 128)
    pieces = buffer(2, NT, NZ, PART, 8, 128)
    single = buffer(2, NT, PART, 8, 128)
    grid = buffer(NL, NT, NF, 8, CHUNK)
    constants = [jnp.asarray(t) for t in tables()]
    flat = jax.ShapeDtypeStruct((NL, NX, LANES), F32)
    many = dma((2, NT, NF))
    few = dma((2, NT))
    return pl.pallas_call(
        kernel,
        out_shape=(flat, flat),
        in_specs=[vmem] * (3 + len(constants)),
        out_specs=(vmem, vmem),
        scratch_shapes=[
            buffer(NG, CHUNK), buffer(NT, NZ, 9, 8, 128), tiles, tiles, planes, planes,
            buffer(PLANES, 128), planes, planes, grid, grid, grid, grid,
            pieces, pieces, pieces, single, single, pieces, pieces,
            many, many, many, many, few, few, few, few, many, many, many, many, many, many,
        ],
        compiler_params=pltpu.CompilerParams(
            collective_id=0, has_side_effects=True, vmem_limit_bytes=60 << 20
        ),
    )(orbitals, keep, cutoff_mask, *constants)


def solution(mesh):
    in_specs = (P("band", "fft", None), P(), P(None, "fft"))
    out_specs = (P("band", "fft", None), P(None, "fft", None))
    return jax.shard_map(
        per_device, mesh=mesh, in_specs=in_specs, out_specs=out_specs, check_vma=False
    )
```

time: 1010 us -> 116 us (0.11)
  waiting for transfers between devices: 565 us -> 0 us
  other arithmetic: 201 us -> 0 us
  local copies, waits for them, and re-layouts: 136 us -> 7.59 us
  Pallas kernels: 0 us -> 107 us
  blocking collectives: 39.7 us -> 0 us
  matrix products: 23.2 us -> 0 us
  starting transfers between devices: 14 us -> 0 us
  between operations: 15.3 us -> 1.3 us
  loops' own time: 12.6 us -> 0 us
    psum x2 -> x0, waiting for transfers between devices: 536 us -> none  [the longest x1 269 us: per_device(): block_total = lax.psum(block_terms, 'band')]
    while x5 -> x0, other arithmetic: 178 us -> none
    pallas_call x0 -> x1, Pallas kernels: none -> 107 us  [per_device(): pl.pallas_call(kernel, out_shape=(flat, flat), in_specs=[vmem] * (3 + len...]
    while x16 -> x0, local copies, waits for them, and re-layouts: 86.9 us -> none
    all_to_all x4 -> x0, blocking collectives: 39.7 us -> none  [one_pair(): lax.all_to_all(single[None], 'fft', split_axis=3, concat_axis=2, tiled=True)]
    all_to_all x4 -> x0, waiting for transfers between devices: 28.1 us -> none  [one_pair(): lax.all_to_all(pencil_out, 'fft', split_axis=2, concat_axis=3, tiled=True)]
    dot_general x12 -> x0, matrix products: 23.2 us -> none  [transform_dim(): return jnp.einsum(pattern, values, matrix, precision=lax.Precision.HIGHEST)]
    all_to_all x16 -> x0, local copies, waits for them, and re-layouts: 16.1 us -> none  [the longest x12 15.9 us: one_pair(): lax.all_to_all(single[None], 'fft', split_axis=3, concat_axis=2, tiled=True)]
  transfers between devices with their start and end apart: 6 -> 0, of which waited for: 6 -> 0; matrix products, arithmetic and copies ran while one was open for 0% -> 0% of each run, Pallas kernels for 0% -> 0%
where the time goes in v2:
time: 116 us
  Pallas kernels  107 us (92%)
  local copies, waits for them, and re-layouts  7.59 us (7%)
  between operations  1.3 us (1%)
    pallas_call x1, Pallas kernels, per_device(): pl.pallas_call(kernel, out_shape=(flat, flat), in_specs=[vmem] * (3 + len...  107 us
    pallas_call x2, local copies, waits for them, and re-layouts, per_device(): pl.pallas_call(kernel, out_shape=(flat, flat), in_specs=[vmem] * (3 + len...  4.56 us
    unnamed x3, local copies, waits for them, and re-layouts  2.44 us

profile of v2, /device:TPU:1, one launch (start us, length us, event | category | flops | bytes accessed | tf_op | source)
XLA Modules:
  0.0 115.6 jit_solution(11547871889985130810)
XLA Ops:
  1.3 0.6 broadcast_in_dim.3.keep_ref
  1.9 2.4 %copy.12.orb_ref = f32[2,12,9216]{2,1,0:T(8,128)} copy(f32[2,12,9216]{2,0,1:T(2,128)} %param.10) | data formatting | bytes 1769472 | tf_op args[0]
  4.3 106.7 %shard_map.113 = (f32[2,12,9216]{2,1,0:T(8,128)}, f32[2,12,9216]{2,1,0:T(8,128)}) custom-call(f32[2,12,9216]{2,1,0:T(8,128)} %copy.12.orb_ref, f32[8,128]{1,0:T(8,128)} %broadcast_in_dim.3.keep_ref, s32[96,1152]{1,0:T(8,128)} %mask_ref.1, bf16[192,192]{1,0:T(8,128)(2,1)} %constant.20.clone.left_y, bf16[256,256]{1,0:T(8,128)(2,1)} %constant.21.clone.right_z, ...), custom_call_target="tpu_custom_call" | custom-call | tf_op jit(solution)/shard_map/pallas_call | solution.py:476
  111.0 0.0 copy-start
  111.1 3.0 %copy.13 = f32[2,12,9216]{2,0,1:T(2,128)} copy(f32[2,12,9216]{2,1,0:T(8,128)} %get-tuple-element.2) | data formatting | bytes 1769472 | tf_op jit(solution)/shard_map/pallas_call | solution.py:476
  114.0 0.0 copy-done
  114.0 1.6 %copy.14 = f32[2,12,9216]{2,0,1:T(2,128)} copy(f32[2,12,9216]{2,1,0:T(8,128)S(1)} %copy-done) | data formatting | bytes 1769472 | tf_op jit(solution)/shard_map/pallas_call | solution.py:476
Async XLA Ops:
  111.0 3.0 %copy-start = (f32[2,12,9216]{2,1,0:T(8,128)S(1)}, f32[2,12,9216]{2,1,0:T(8,128)}, u32[]{:S(2)}) copy-start(f32[2,12,9216]{2,1,0:T(8,128)} %get-tuple-element.3) | copy-start | bytes 2654212

commit v3 on v2

--- a/solution.py
+++ b/solution.py
@@ -47,9 +47,9 @@
     right_z[:NG, :NG] = cas_h
     right_z[128 : 128 + NG, :NG] = cas_h
     right_z[:NG, 128 : 128 + NG] = cas_l
-    both = np.zeros((NL, NG, NT, NF, NL, 4))
+    both = np.zeros((NL, NG, NT, NF, 4, NL))
     for i in range(NL):
-        both[i, :, :, :, i, :] = cas.reshape(NG, NF, NT, 4).transpose(0, 2, 1, 3)
+        both[i, :, :, :, :, i] = cas.reshape(NG, NF, NT, 4).transpose(0, 2, 1, 3)
     both = both.reshape(NL * NG, NL * NG)
     left_fx = np.concatenate(split_const(both), 0)
     left_bx = np.concatenate(split_const(both.T), 0)
@@ -104,7 +104,7 @@
 
 
 def kernel(
-    orb_ref, keep_ref, mask_ref, left_y, right_z, left_fx, left_bx, lane_y, lane_z, row_x,
+    orb_ref, owner_ref, mask_ref, left_y, right_z, left_fx, left_bx, lane_y, lane_z, row_x,
     local_ref, block_ref,
     coulomb, orb_t, source, full, orb_u, blk_u, turned, local_u, block_u,
     send_a, recv_a, send_b, recv_b, pair, part, gathered, summed, other, total, mate,
@@ -229,14 +229,14 @@
 
         lax.fori_loop(0, NZ, step, 0, unroll=2)
 
+    mine = jnp.broadcast_to(owner_ref[0], (8, 128)) == band
+
     def load_tiles(c, _):
         lanes = pl.ds(pl.multiple_of(c * 128, 128), 128)
-        rows0, rows1 = orb_ref[0, :, lanes], orb_ref[1, :, lanes]
-        keep = keep_ref[...]
         for t in range(NT):
-            tile = jnp.concatenate([rows0[4 * t : 4 * t + 4], rows1[4 * t : 4 * t + 4]], axis=0)
+            tile = orb_ref[4 * t : 4 * t + 4, :, lanes].reshape(8, 128)
             orb_t[t, c // 9, c % 9] = tile
-            source[0, t, c // 9, c % 9] = tile * keep
+            source[0, t, c // 9, c % 9] = jnp.where(mine, tile, 0.0)
         return 0
 
     lax.fori_loop(0, LANES // 128, load_tiles, 0, unroll=4)
@@ -270,7 +270,6 @@
     lax.fori_loop(0, QUADS, open_orb, 0, unroll=2)
     for t in range(NT):
         sum_c(0, t)
-    for t in range(NT):
         sum_d(0, t)
 
     def open_blk(t):
@@ -295,12 +294,12 @@
 
     def forward(j, t):
         def rows(s, _):
-            blk = blk_u[t, across(4 * j + s), :]
+            blk = blk_u[t, across(2 * s + j), :]
             out0, out1 = transform_y(
-                orb_u[t, across(s), :] * blk, orb_u[t, across(4 + s), :] * blk
+                orb_u[t, across(2 * s), :] * blk, orb_u[t, across(2 * s + 1), :] * blk
             )
-            turned[across(s), :] = out0
-            turned[across(4 + s), :] = out1
+            turned[across(2 * s), :] = out0
+            turned[across(2 * s + 1), :] = out1
             return 0
 
         lax.fori_loop(0, 4, rows, 0, unroll=2)
@@ -363,16 +362,17 @@
         lax.fori_loop(0, 2, half, 0)
 
         def rows(s, _):
-            pot0, pot1 = transform_y(turned[across(s), :], turned[across(4 + s), :])
-            blk = blk_u[t, across(4 * j + s), :]
+            even, odd = across(2 * s), across(2 * s + 1)
+            pot0, pot1 = transform_y(turned[even, :], turned[odd, :])
+            blk = blk_u[t, across(2 * s + j), :]
             term0, term1 = blk * pot0, blk * pot1
             if j > 0:
-                term0 = local_u[t, across(s), :] + term0
-                term1 = local_u[t, across(4 + s), :] + term1
-            local_u[t, across(s), :] = term0
-            local_u[t, across(4 + s), :] = term1
-            block_u[t, across(4 * j + s), :] = (
-                orb_u[t, across(s), :] * pot0 + orb_u[t, across(4 + s), :] * pot1
+                term0 = local_u[t, even, :] + term0
+                term1 = local_u[t, odd, :] + term1
+            local_u[t, even, :] = term0
+            local_u[t, odd, :] = term1
+            block_u[t, across(2 * s + j), :] = (
+                orb_u[t, even, :] * pot0 + orb_u[t, odd, :] * pot1
             )
             return 0
 
@@ -389,8 +389,7 @@
 
     def write(ref, t, column, tile):
         lanes = pl.ds(pl.multiple_of(column * 128, 128), 128)
-        ref[0, 4 * t : 4 * t + 4, lanes] = tile[:4]
-        ref[1, 4 * t : 4 * t + 4, lanes] = tile[4:]
+        ref[4 * t : 4 * t + 4, :, lanes] = tile.reshape(4, NL, 128)
 
     def write_local(a, _):
         for t in range(NT):
@@ -417,25 +416,15 @@
     middle(1)
     for t in range(NT):
         backward(0, t)
-    backward(1, 0)
-    close_block(0)
-    sum_a(1, 0)
-    backward(1, 1)
-    close_block(1)
-    sum_a(1, 1)
-    sum_b(1, 0)
-    backward(1, 2)
-    close_block(2)
-    sum_a(1, 2)
-    sum_b(1, 1)
-    sum_c(1, 0)
-    sum_b(1, 2)
+    for t in range(NT):
+        backward(1, t)
+        close_block(t)
+        sum_a(1, t)
+        sum_b(1, t)
     lax.fori_loop(0, QUADS, write_local, 0, unroll=2)
-    sum_d(1, 0)
-    sum_c(1, 1)
-    sum_d(1, 1)
-    sum_c(1, 2)
-    sum_d(1, 2)
+    for t in range(NT):
+        sum_c(1, t)
+        sum_d(1, t)
     for t in range(NT):
         sum_e(1, t)
     for t in range(NT):
@@ -456,8 +445,6 @@
 
 
 def per_device(orbitals, owners, cutoff_mask):
-    mine = lax.axis_index("band") == owners[0]
-    keep = jnp.broadcast_to(mine.astype(F32), (8, 128))
     vmem = pl.BlockSpec(memory_space=pltpu.VMEM)
     dma = pltpu.SemaphoreType.DMA
 
@@ -470,13 +457,13 @@
     single = buffer(2, NT, PART, 8, 128)
     grid = buffer(NL, NT, NF, 8, CHUNK)
     constants = [jnp.asarray(t) for t in tables()]
-    flat = jax.ShapeDtypeStruct((NL, NX, LANES), F32)
+    flat = jax.ShapeDtypeStruct((NX, NL, LANES), F32)
     many = dma((2, NT, NF))
     few = dma((2, NT))
-    return pl.pallas_call(
+    local, block = pl.pallas_call(
         kernel,
         out_shape=(flat, flat),
-        in_specs=[vmem] * (3 + len(constants)),
+        in_specs=[vmem, pl.BlockSpec(memory_space=pltpu.SMEM)] + [vmem] * (1 + len(constants)),
         out_specs=(vmem, vmem),
         scratch_shapes=[
             buffer(NG, CHUNK), buffer(NT, NZ, 9, 8, 128), tiles, tiles, planes, planes,
@@ -487,7 +474,8 @@
         compiler_params=pltpu.CompilerParams(
             collective_id=0, has_side_effects=True, vmem_limit_bytes=60 << 20
         ),
-    )(orbitals, keep, cutoff_mask, *constants)
+    )(orbitals.transpose(1, 0, 2), owners, cutoff_mask, *constants)
+    return local.transpose(1, 0, 2), block.transpose(1, 0, 2)
 
 
 def solution(mesh):

time: 116 us -> 107 us (0.922)
  Pallas kernels: 107 us -> 102 us
  local copies, waits for them, and re-layouts: 7.59 us -> 3.13 us
    pallas_call x2 -> x0, local copies, waits for them, and re-layouts: 4.56 us -> none  [per_device(): pl.pallas_call(kernel, out_shape=(flat, flat), in_specs=[vmem] * (3 + len...]
    pallas_call x1, Pallas kernels: 107 us -> 102 us  [per_device(): pl.pallas_call(kernel, out_shape=(flat, flat), in_specs=[vmem, pl.BlockSp...]
    unnamed x3 -> x4, local copies, waits for them, and re-layouts: 2.44 us -> 3.13 us
where the time goes in v3:
time: 107 us
  Pallas kernels  102 us (95%)
  local copies, waits for them, and re-layouts  3.13 us (3%)
  between operations  1.29 us (1%)
    pallas_call x1, Pallas kernels, per_device(): pl.pallas_call(kernel, out_shape=(flat, flat), in_specs=[vmem, pl.BlockSp...  102 us
    unnamed x4, local copies, waits for them, and re-layouts  3.13 us

profile of v3, /device:TPU:1, one launch (start us, length us, event | category | flops | bytes accessed | tf_op | source)
XLA Modules:
  0.0 106.7 jit_solution(1212250946400731432)
XLA Ops:
  1.3 102.3 %shard_map.113 = (f32[12,2,9216]{2,1,0:T(2,128)}, f32[12,2,9216]{2,1,0:T(2,128)}) custom-call(f32[12,2,9216]{2,1,0:T(2,128)} %bitcast.3, s32[1]{0:T(128)S(6)} %copy.14.owner_ref, s32[96,1152]{1,0:T(8,128)} %mask_ref.1, bf16[192,192]{1,0:T(8,128)(2,1)} %constant.14.clone.left_y, bf16[256,256]{1,0:T(8,128)(2,1)} %constant.15.clone.right_z, ...), custom_call_target="tpu_custom_call" | custom-call | tf_op jit(solution)/shard_map/pallas_call | solution.py:463
  103.5 0.0 copy-start
  103.6 2.2 %copy.15 = f32[2,12,9216]{2,0,1:T(2,128)} copy(f32[2,12,9216]{2,0,1:T(2,128)} %bitcast.5) | data formatting | bytes 1769472
  105.8 0.0 copy-done
  105.8 0.9 copy.16
Async XLA Ops:
  103.5 2.2 %copy-start = (f32[12,2,9216]{2,1,0:T(2,128)S(1)}, f32[12,2,9216]{2,1,0:T(2,128)}, u32[]{:S(2)}) copy-start(f32[12,2,9216]{2,1,0:T(2,128)} %get-tuple-element.5) | copy-start | bytes 2654212

commit v4 on v3

--- a/solution.py
+++ b/solution.py
@@ -78,14 +78,14 @@
 
 
 def open_quad(c0, c1, c2):
-    lane = lax.broadcasted_iota(jnp.int32, (8, 128), 1)
+    lane = lax.broadcasted_iota(jnp.int32, c0.shape, 1)
     y1 = jnp.where(lane < 32, pltpu.roll(c0, 32, 1), pltpu.roll(c1, 32, 1))
     y2 = jnp.where(lane < 64, pltpu.roll(c1, 64, 1), pltpu.roll(c2, 64, 1))
     return c0, y1, y2, pltpu.roll(c2, 96, 1)
 
 
 def close_quad(e0, e1, e2, e3):
-    lane = lax.broadcasted_iota(jnp.int32, (8, 128), 1)
+    lane = lax.broadcasted_iota(jnp.int32, e0.shape, 1)
     r1 = pltpu.roll(e1, 96, 1)
     r2 = pltpu.roll(e2, 64, 1)
     r3 = pltpu.roll(e3, 32, 1)
@@ -104,9 +104,11 @@
 
 
 def kernel(
-    orb_ref, owner_ref, mask_ref, left_y, right_z, left_fx, left_bx, lane_y, lane_z, row_x,
-    local_ref, block_ref,
-    coulomb, orb_t, source, full, orb_u, blk_u, turned, local_u, block_u,
+    orb_hbm, owner_ref, mask_hbm, left_y_hbm, right_z_hbm, left_fx_hbm, left_bx_hbm,
+    lane_y_hbm, lane_z_hbm, row_x_hbm, local_hbm, block_hbm,
+    orb_ref, mask_ref, left_y, right_z, left_fx, left_bx, lane_y, lane_z, row_x,
+    local_ref, block_ref, in_sem, out_sem,
+    coulomb, source, full, orb_u, blk_u, turned, local_u, block_u,
     send_a, recv_a, send_b, recv_b, pair, part, gathered, summed, other, total, mate,
     sa_sem, ra_sem, sb_sem, rb_sem, ps_sem, pr_sem, ys_sem, yr_sem,
     zs_sem, zr_sem, gs_sem, gr_sem, ms_sem, mr_sem,
@@ -128,6 +130,16 @@
     def turn_z(o):
         return lax.rem(z + o, NZ)
 
+    inputs = (
+        (orb_hbm, orb_ref), (mask_hbm, mask_ref), (left_y_hbm, left_y), (right_z_hbm, right_z),
+        (left_fx_hbm, left_fx), (left_bx_hbm, left_bx), (lane_y_hbm, lane_y),
+        (lane_z_hbm, lane_z), (row_x_hbm, row_x),
+    )
+    fetches = [
+        pltpu.make_async_copy(src, dst, in_sem.at[n]) for n, (src, dst) in enumerate(inputs)
+    ]
+    for fetch in fetches:
+        fetch.start()
     barrier = pltpu.get_barrier_semaphore()
     devices = [{"fft": turn(o)} for o in range(1, NF)]
     devices += [{"band": mate_band}, {"band": y_band}]
@@ -153,98 +165,106 @@
             sb_sem.at[j, t, peer], rb_sem.at[j, t, slot], {"fft": peer},
         )
 
-    def to_pair(q, t):
-        return remote(
-            source.at[q, t, :, pl.ds(4 * (1 - core), PART)], pair.at[q, t],
-            ps_sem.at[q, t], pr_sem.at[q, t], {"band": mate_band},
-        )
-
-    def scatter(q, t, peer, slot):
-        return remote(
-            part.at[q, t, peer], gathered.at[q, t, slot],
-            zs_sem.at[q, t, peer], zr_sem.at[q, t, slot], {"band": z_band(peer)},
-        )
-
-    def to_y(q, t):
-        return remote(
-            summed.at[q, t], other.at[q, t], ys_sem.at[q, t], yr_sem.at[q, t], {"band": y_band}
-        )
-
-    def spread(q, t, peer, slot):
-        return remote(
-            total.at[q, t, slot], total.at[q, t, slot],
-            gs_sem.at[q, t, peer], gr_sem.at[q, t, slot], {"band": z_band(peer)},
-        )
-
-    def to_mate(q, t, slot):
-        return remote(
-            total.at[q, t, slot], mate.at[q, t, slot],
-            ms_sem.at[q, t, slot], mr_sem.at[q, t, slot], {"band": mate_band},
-        )
-
-    def sum_a(q, t):
-        to_pair(q, t).start()
-
-    def sum_b(q, t):
-        to_pair(q, t).wait_recv()
+    def to_pair(q, j, t):
+        return remote(
+            source.at[q, j, t, :, pl.ds(4 * (1 - core), PART)], pair.at[q, j, t],
+            ps_sem.at[q, j, t], pr_sem.at[q, j, t], {"band": mate_band},
+        )
+
+    def scatter(q, j, t, peer, slot):
+        return remote(
+            part.at[q, j, t, peer], gathered.at[q, j, t, slot],
+            zs_sem.at[q, j, t, peer], zr_sem.at[q, j, t, slot], {"band": z_band(peer)},
+        )
+
+    def to_y(q, j, t):
+        return remote(
+            summed.at[q, j, t], other.at[q, j, t],
+            ys_sem.at[q, j, t], yr_sem.at[q, j, t], {"band": y_band},
+        )
+
+    def spread(q, j, t, peer, slot):
+        return remote(
+            total.at[q, j, t, slot], total.at[q, j, t, slot],
+            gs_sem.at[q, j, t, peer], gr_sem.at[q, j, t, slot], {"band": z_band(peer)},
+        )
+
+    def to_mate(q, j, t, slot):
+        return remote(
+            total.at[q, j, t, slot], mate.at[q, j, t, slot],
+            ms_sem.at[q, j, t, slot], mr_sem.at[q, j, t, slot], {"band": mate_band},
+        )
+
+    def sum_a(q, j, t):
+        to_pair(q, j, t).start()
+
+    def sum_b(q, j, t):
+        to_pair(q, j, t).wait_recv()
 
         def step(k, _):
-            part[q, t, k] = source[q, t, k, pl.ds(4 * core, PART)] + pair[q, t, k]
+            part[q, j, t, k] = source[q, j, t, k, pl.ds(4 * core, PART)] + pair[q, j, t, k]
             return 0
 
         lax.fori_loop(0, NZ, step, 0, unroll=2)
         for o in FAR:
-            scatter(q, t, turn_z(o), z).start()
-        gathered[q, t, z] = part[q, t, z]
-
-    def sum_c(q, t):
+            scatter(q, j, t, turn_z(o), z).start()
+        gathered[q, j, t, z] = part[q, j, t, z]
+
+    def sum_c(q, j, t):
         for o in FAR:
-            scatter(q, t, turn_z(o), turn_z(o)).wait_recv()
-        value = gathered[q, t, 0]
+            scatter(q, j, t, turn_z(o), turn_z(o)).wait_recv()
+        value = gathered[q, j, t, 0]
         for k in range(1, NZ):
-            value = value + gathered[q, t, k]
-        summed[q, t] = value
-        to_y(q, t).start()
-
-    def sum_d(q, t):
-        to_y(q, t).wait_recv()
-        total[q, t, z] = summed[q, t] + other[q, t]
+            value = value + gathered[q, j, t, k]
+        summed[q, j, t] = value
+        to_y(q, j, t).start()
+
+    def sum_d(q, j, t):
+        to_y(q, j, t).wait_recv()
+        total[q, j, t, z] = summed[q, j, t] + other[q, j, t]
         for o in FAR:
-            spread(q, t, turn_z(o), z).start()
-        to_mate(q, t, z).start()
-
-    def sum_e(q, t):
+            spread(q, j, t, turn_z(o), z).start()
+        to_mate(q, j, t, z).start()
+
+    def sum_e(q, j, t):
         for o in NEAR:
-            spread(q, t, turn_z(o), turn_z(o)).wait_recv()
-            to_mate(q, t, turn_z(o)).start()
-
-    def sum_f(q, t):
+            spread(q, j, t, turn_z(o), turn_z(o)).wait_recv()
+            to_mate(q, j, t, turn_z(o)).start()
+
+    def sum_f(q, j, t):
         for o in (0,) + NEAR:
-            to_mate(q, t, turn_z(o)).wait_recv()
+            to_mate(q, j, t, turn_z(o)).wait_recv()
 
         def step(k, _):
-            full[q, t, k, pl.ds(4 * core, PART)] = total[q, t, k]
-            full[q, t, k, pl.ds(4 * (1 - core), PART)] = mate[q, t, k]
+            full[q, j, t, k, pl.ds(4 * core, PART)] = total[q, j, t, k]
+            full[q, j, t, k, pl.ds(4 * (1 - core), PART)] = mate[q, j, t, k]
             return 0
 
         lax.fori_loop(0, NZ, step, 0, unroll=2)
 
-    mine = jnp.broadcast_to(owner_ref[0], (8, 128)) == band
+    mine = jnp.broadcast_to(owner_ref[0], (4, 128)) == band
 
     def load_tiles(c, _):
         lanes = pl.ds(pl.multiple_of(c * 128, 128), 128)
         for t in range(NT):
-            tile = orb_ref[4 * t : 4 * t + 4, :, lanes].reshape(8, 128)
-            orb_t[t, c // 9, c % 9] = tile
-            source[0, t, c // 9, c % 9] = jnp.where(mine, tile, 0.0)
+            tile = orb_ref[4 * t : 4 * t + 4, :, lanes]
+            for j in range(NL):
+                source[0, j, t, c // 9, c % 9] = jnp.where(mine, tile[:, j, :], 0.0)
         return 0
 
+    fetches[0].wait()
     lax.fori_loop(0, LANES // 128, load_tiles, 0, unroll=4)
     pl.semaphore_wait(barrier, len(devices))
+    for j in range(NL):
+        for t in range(NT):
+            sum_a(0, j, t)
     for t in range(NT):
-        sum_a(0, t)
-
-    low = lax.rem(me, NF) * NX + lane_y[...]
+        sum_b(0, 0, t)
+    sum_b(0, 1, 0)
+    for fetch in fetches[1:]:
+        fetch.wait()
+
+    low = me * NX + lane_y[...]
     low = jnp.where(low <= NG // 2, low, low - NG)
     flat = low * low + lane_z[...]
 
@@ -257,26 +277,28 @@
         return 0
 
     lax.fori_loop(0, NG // 8, coulomb_rows, 0)
-    for t in range(NT):
-        sum_b(0, t)
 
     def open_orb(a, _):
         for t in range(NT):
-            quad = open_quad(*[orb_t[t, a // 3, (a % 3) * 3 + k] for k in range(3)])
+            tiles = []
+            for k in range(3):
+                lanes = pl.ds(pl.multiple_of(a * 384 + 128 * k, 128), 128)
+                tiles.append(orb_ref[4 * t : 4 * t + 4, :, lanes].reshape(8, 128))
+            quad = open_quad(*tiles)
             for b in range(4):
                 orb_u[t, plane(4 * a + b), :] = quad[b]
         return 0
 
     lax.fori_loop(0, QUADS, open_orb, 0, unroll=2)
-    for t in range(NT):
-        sum_c(0, t)
-        sum_d(0, t)
-
-    def open_blk(t):
+
+    def half_plane(y, j):
+        return pl.ds(y * 8 + 4 * j, 4)
+
+    def open_blk(j, t):
         def step(a, _):
-            quad = open_quad(*[full[0, t, a // 3, (a % 3) * 3 + k] for k in range(3)])
+            quad = open_quad(*[full[0, j, t, a // 3, (a % 3) * 3 + k] for k in range(3)])
             for b in range(4):
-                blk_u[t, plane(4 * a + b), :] = quad[b]
+                blk_u[t, half_plane(4 * a + b, j), :] = quad[b]
             return 0
 
         lax.fori_loop(0, QUADS, step, 0, unroll=4)
@@ -294,7 +316,7 @@
 
     def forward(j, t):
         def rows(s, _):
-            blk = blk_u[t, across(2 * s + j), :]
+            blk = blk_u[t, across(4 * j + s), :]
             out0, out1 = transform_y(
                 orb_u[t, across(2 * s), :] * blk, orb_u[t, across(2 * s + 1), :] * blk
             )
@@ -364,117 +386,179 @@
         def rows(s, _):
             even, odd = across(2 * s), across(2 * s + 1)
             pot0, pot1 = transform_y(turned[even, :], turned[odd, :])
-            blk = blk_u[t, across(2 * s + j), :]
+            blk = blk_u[t, across(4 * j + s), :]
             term0, term1 = blk * pot0, blk * pot1
             if j > 0:
                 term0 = local_u[t, even, :] + term0
                 term1 = local_u[t, odd, :] + term1
             local_u[t, even, :] = term0
             local_u[t, odd, :] = term1
-            block_u[t, across(2 * s + j), :] = (
+            block_u[t, across(4 * j + s), :] = (
                 orb_u[t, even, :] * pot0 + orb_u[t, odd, :] * pot1
             )
             return 0
 
         lax.fori_loop(0, 4, rows, 0, unroll=2)
 
-    def close_block(t):
+    def close_block(j, t):
         def step(a, _):
-            tiles = close_quad(*[block_u[t, plane(4 * a + b), :] for b in range(4)])
+            tiles = close_quad(*[block_u[t, half_plane(4 * a + b, j), :] for b in range(4)])
             for k in range(3):
-                source[1, t, a // 3, (a % 3) * 3 + k] = tiles[k]
+                source[1, j, t, a // 3, (a % 3) * 3 + k] = tiles[k]
             return 0
 
         lax.fori_loop(0, QUADS, step, 0, unroll=4)
-
-    def write(ref, t, column, tile):
-        lanes = pl.ds(pl.multiple_of(column * 128, 128), 128)
-        ref[4 * t : 4 * t + 4, :, lanes] = tile.reshape(4, NL, 128)
 
     def write_local(a, _):
         for t in range(NT):
             tiles = close_quad(*[local_u[t, plane(4 * a + b), :] for b in range(4)])
             for k in range(3):
-                write(local_ref, t, 3 * a + k, tiles[k])
+                lanes = pl.ds(pl.multiple_of(a * 384 + 128 * k, 128), 128)
+                local_ref[4 * t : 4 * t + 4, :, lanes] = tiles[k].reshape(4, NL, 128)
         return 0
 
-    def write_block(t):
+    def write_block(j, t):
         def step(c, _):
-            write(block_ref, t, c, full[1, t, c // 9, c % 9])
+            lanes = pl.ds(pl.multiple_of(c * 128, 128), 128)
+            block_ref[4 * t : 4 * t + 4, j, lanes] = full[1, j, t, c // 9, c % 9]
             return 0
 
         lax.fori_loop(0, LANES // 128, step, 0, unroll=4)
 
-    for t in range(NT):
-        sum_e(0, t)
-        sum_f(0, t)
-        open_blk(t)
-        forward(0, t)
-    for t in range(NT):
-        forward(1, t)
+    def receive(j, t):
+        sum_e(0, j, t)
+        sum_f(0, j, t)
+        open_blk(j, t)
+        forward(j, t)
+
+    def finish(j, t):
+        sum_e(1, j, t)
+        sum_f(1, j, t)
+        write_block(j, t)
+
+    def block_out(t):
+        return pltpu.make_async_copy(
+            block_ref.at[pl.ds(4 * t, 4)], block_hbm.at[pl.ds(4 * t, 4)], out_sem.at[t]
+        )
+
+    sum_c(0, 0, 0)
+    sum_c(0, 0, 1)
+    sum_c(0, 0, 2)
+    sum_d(0, 0, 0)
+    sum_b(0, 1, 1)
+    sum_c(0, 1, 0)
+    sum_d(0, 0, 1)
+    sum_b(0, 1, 2)
+    sum_d(0, 0, 2)
+    sum_d(0, 1, 0)
+    receive(0, 0)
+    sum_c(0, 1, 1)
+    receive(0, 1)
+    sum_d(0, 1, 1)
+    sum_c(0, 1, 2)
+    receive(0, 2)
+    sum_d(0, 1, 2)
+    receive(1, 0)
+    receive(1, 1)
+    receive(1, 2)
     middle(0)
     middle(1)
+
+    def back(j, t):
+        backward(j, t)
+        close_block(j, t)
+        sum_a(1, j, t)
+
+    back(0, 0)
+    sum_b(1, 0, 0)
+    back(0, 1)
+    sum_b(1, 0, 1)
+    back(0, 2)
+    sum_b(1, 0, 2)
+    sum_c(1, 0, 0)
+    back(1, 0)
+    sum_b(1, 1, 0)
+    sum_c(1, 0, 1)
+    sum_d(1, 0, 0)
+    back(1, 1)
+    sum_b(1, 1, 1)
+    sum_c(1, 0, 2)
+    sum_d(1, 0, 1)
+    back(1, 2)
+    sum_c(1, 1, 0)
+    sum_d(1, 0, 2)
+    sum_b(1, 1, 2)
+    lax.fori_loop(0, QUADS, write_local, 0, unroll=2)
+    local_out = pltpu.make_async_copy(local_ref, local_hbm, out_sem.at[NT])
+    local_out.start()
+    sum_c(1, 1, 1)
+    sum_d(1, 1, 0)
+    finish(0, 0)
+    sum_d(1, 1, 1)
+    finish(0, 1)
+    sum_c(1, 1, 2)
+    finish(0, 2)
+    sum_d(1, 1, 2)
     for t in range(NT):
-        backward(0, t)
-    for t in range(NT):
-        backward(1, t)
-        close_block(t)
-        sum_a(1, t)
-        sum_b(1, t)
-    lax.fori_loop(0, QUADS, write_local, 0, unroll=2)
-    for t in range(NT):
-        sum_c(1, t)
-        sum_d(1, t)
-    for t in range(NT):
-        sum_e(1, t)
-    for t in range(NT):
-        sum_f(1, t)
-        write_block(t)
+        finish(1, t)
+        block_out(t).start()
     for t in range(NT):
         for j in range(NL):
             for o in range(1, NF):
                 copy_a(j, t, turn(o), me).wait_send()
                 copy_b(j, t, turn(o), me).wait_send()
-            to_pair(j, t).wait_send()
-            to_y(j, t).wait_send()
-            to_mate(j, t, z).wait_send()
-            for o in range(1, NZ):
-                scatter(j, t, turn_z(o), z).wait_send()
-                spread(j, t, turn_z(o), z).wait_send()
-                to_mate(j, t, turn_z(o)).wait_send()
+            for q in range(2):
+                to_pair(q, j, t).wait_send()
+                to_y(q, j, t).wait_send()
+                to_mate(q, j, t, z).wait_send()
+                for o in range(1, NZ):
+                    scatter(q, j, t, turn_z(o), z).wait_send()
+                    spread(q, j, t, turn_z(o), z).wait_send()
+                    to_mate(q, j, t, turn_z(o)).wait_send()
+    local_out.wait()
+    for t in range(NT):
+        block_out(t).wait()
 
 
 def per_device(orbitals, owners, cutoff_mask):
-    vmem = pl.BlockSpec(memory_space=pltpu.VMEM)
     dma = pltpu.SemaphoreType.DMA
 
     def buffer(*shape):
         return pltpu.VMEM(shape, F32)
 
+    def like(array):
+        return pltpu.VMEM(array.shape, array.dtype)
+
     planes = buffer(NT, PLANES, 128)
-    tiles = buffer(2, NT, NZ, 9, 8, 128)
-    pieces = buffer(2, NT, NZ, PART, 8, 128)
-    single = buffer(2, NT, PART, 8, 128)
+    tiles = buffer(2, NL, NT, NZ, 9, 4, 128)
+    pieces = buffer(2, NL, NT, NZ, PART, 4, 128)
+    single = buffer(2, NL, NT, PART, 4, 128)
     grid = buffer(NL, NT, NF, 8, CHUNK)
     constants = [jnp.asarray(t) for t in tables()]
     flat = jax.ShapeDtypeStruct((NX, NL, LANES), F32)
-    many = dma((2, NT, NF))
-    few = dma((2, NT))
+    many = dma((NL, NT, NF))
+    bulk = dma((2, NL, NT, NZ))
+    few = dma((2, NL, NT))
+    anywhere = pl.BlockSpec(memory_space=pl.ANY)
+    orb = orbitals.transpose(1, 0, 2)
     local, block = pl.pallas_call(
         kernel,
         out_shape=(flat, flat),
-        in_specs=[vmem, pl.BlockSpec(memory_space=pltpu.SMEM)] + [vmem] * (1 + len(constants)),
-        out_specs=(vmem, vmem),
+        in_specs=[anywhere, pl.BlockSpec(memory_space=pltpu.SMEM)]
+        + [anywhere] * (1 + len(constants)),
+        out_specs=(anywhere, anywhere),
         scratch_shapes=[
-            buffer(NG, CHUNK), buffer(NT, NZ, 9, 8, 128), tiles, tiles, planes, planes,
+            like(orb), like(cutoff_mask), *[like(c) for c in constants],
+            like(flat), like(flat), dma((2 + len(constants),)), dma((NT + 1,)),
+            buffer(NG, CHUNK), tiles, tiles, planes, planes,
             buffer(PLANES, 128), planes, planes, grid, grid, grid, grid,
             pieces, pieces, pieces, single, single, pieces, pieces,
-            many, many, many, many, few, few, few, few, many, many, many, many, many, many,
+            many, many, many, many, few, few, few, few, bulk, bulk, bulk, bulk, bulk, bulk,
         ],
         compiler_params=pltpu.CompilerParams(
             collective_id=0, has_side_effects=True, vmem_limit_bytes=60 << 20
         ),
-    )(orbitals.transpose(1, 0, 2), owners, cutoff_mask, *constants)
+    )(orb, owners, cutoff_mask, *constants)
     return local.transpose(1, 0, 2), block.transpose(1, 0, 2)
 
 

time: 107 us -> 107 us (level)
  no operation moved by 1% of the time
where the time goes in v4:
time: 107 us
  Pallas kernels  102 us (95%)
  local copies, waits for them, and re-layouts  3.13 us (3%)
  between operations  1.29 us (1%)
    pallas_call x1, Pallas kernels, per_device(): pl.pallas_call(kernel, out_shape=(flat, flat), in_specs=[anywhere, pl.Blo...  102 us
    unnamed x4, local copies, waits for them, and re-layouts  3.13 us

profile of v4, /device:TPU:1, one launch (start us, length us, event | category | flops | bytes accessed | tf_op | source)
XLA Modules:
  0.0 106.5 jit_solution(2200726260016002422)
XLA Ops:
  1.3 102.1 %shard_map.113 = (f32[12,2,9216]{2,1,0:T(2,128)}, f32[12,2,9216]{2,1,0:T(2,128)}) custom-call(f32[12,2,9216]{2,1,0:T(2,128)} %bitcast.3, s32[1]{0:T(128)S(6)} %copy.14.owner_ref, s32[96,1152]{1,0:T(8,128)} %mask_hbm.1, bf16[192,192]{1,0:T(8,128)(2,1)} %constant.14.clone.left_y_hbm, bf16[256,256]{1,0:T(8,128)(2,1)} %constant.15.clone.right_z_hbm, ...), custom_call_target="tpu_custom_call" | custom-call | tf_op jit(solution)/shard_map/pallas_call | solution.py:544
  103.4 0.0 copy-start
  103.4 2.2 %copy.15 = f32[2,12,9216]{2,0,1:T(2,128)} copy(f32[2,12,9216]{2,0,1:T(2,128)} %bitcast.5) | data formatting | bytes 1769472
  105.6 0.0 copy-done
  105.6 0.9 copy.16
Async XLA Ops:
  103.4 2.2 %copy-start = (f32[12,2,9216]{2,1,0:T(2,128)S(1)}, f32[12,2,9216]{2,1,0:T(2,128)}, u32[]{:S(2)}) copy-start(f32[12,2,9216]{2,1,0:T(2,128)} %get-tuple-element.5) | copy-start | bytes 2654212

commit v5 on v4

--- a/solution.py
+++ b/solution.py
@@ -25,7 +25,6 @@
 F32 = jnp.float32
 BF16 = jnp.bfloat16
 FAR = (4, 3, 5, 2, 6, 1, 7)
-NEAR = (1, 7, 2, 6, 3, 5, 4)
 
 
 def split_const(matrix):
@@ -53,11 +52,12 @@
     both = both.reshape(NL * NG, NL * NG)
     left_fx = np.concatenate(split_const(both), 0)
     left_bx = np.concatenate(split_const(both.T), 0)
-    signed = np.where(index <= NG // 2, index, index - NG)
-    lane_y = np.tile(np.repeat(np.arange(NX), NG)[None], (8, 1)).astype(np.int32)
-    lane_z = np.tile(np.tile(signed * signed, NX)[None], (8, 1)).astype(np.int32)
-    row_x = np.tile((signed * signed)[:, None], (1, 128)).astype(np.int32)
-    return [left_y, right_z, left_fx, left_bx, lane_y, lane_z, row_x]
+    packed = np.zeros((1216, 256), cas_h.dtype)
+    packed[:192, :192] = left_y
+    packed[192:448] = right_z
+    packed[448:832, :192] = left_fx
+    packed[832:1216, :192] = left_bx
+    return packed
 
 
 def dot(a, b):
@@ -104,9 +104,8 @@
 
 
 def kernel(
-    orb_hbm, owner_ref, mask_hbm, left_y_hbm, right_z_hbm, left_fx_hbm, left_bx_hbm,
-    lane_y_hbm, lane_z_hbm, row_x_hbm, local_hbm, block_hbm,
-    orb_ref, mask_ref, left_y, right_z, left_fx, left_bx, lane_y, lane_z, row_x,
+    orb_hbm, owner_ref, mask_hbm, weights_hbm, local_hbm, block_hbm,
+    orb_ref, mask_ref, weights,
     local_ref, block_ref, in_sem, out_sem,
     coulomb, source, full, orb_u, blk_u, turned, local_u, block_u,
     send_a, recv_a, send_b, recv_b, pair, part, gathered, summed, other, total, mate,
@@ -131,9 +130,7 @@
         return lax.rem(z + o, NZ)
 
     inputs = (
-        (orb_hbm, orb_ref), (mask_hbm, mask_ref), (left_y_hbm, left_y), (right_z_hbm, right_z),
-        (left_fx_hbm, left_fx), (left_bx_hbm, left_bx), (lane_y_hbm, lane_y),
-        (lane_z_hbm, lane_z), (row_x_hbm, row_x),
+        (orb_hbm, orb_ref), (mask_hbm, mask_ref), (weights_hbm, weights),
     )
     fetches = [
         pltpu.make_async_copy(src, dst, in_sem.at[n]) for n, (src, dst) in enumerate(inputs)
@@ -153,16 +150,18 @@
             device_id=device, device_id_type=MESH,
         )
 
+    others = pl.ds(0, NF - 1)
+
     def copy_a(j, t, peer, slot):
         return remote(
             send_a.at[j, t, peer], recv_a.at[j, t, slot],
-            sa_sem.at[j, t, peer], ra_sem.at[j, t, slot], {"fft": peer},
+            sa_sem.at[j, t], ra_sem.at[j, t], {"fft": turn(1) if peer is others else peer},
         )
 
     def copy_b(j, t, peer, slot):
         return remote(
             send_b.at[j, t, peer], recv_b.at[j, t, slot],
-            sb_sem.at[j, t, peer], rb_sem.at[j, t, slot], {"fft": peer},
+            sb_sem.at[j, t], rb_sem.at[j, t], {"fft": turn(1) if peer is others else peer},
         )
 
     def to_pair(q, j, t):
@@ -174,7 +173,8 @@
     def scatter(q, j, t, peer, slot):
         return remote(
             part.at[q, j, t, peer], gathered.at[q, j, t, slot],
-            zs_sem.at[q, j, t, peer], zr_sem.at[q, j, t, slot], {"band": z_band(peer)},
+            zs_sem.at[q, j, t], zr_sem.at[q, j, t],
+            {"band": z_band(turn_z(1) if peer is others else peer)},
         )
 
     def to_y(q, j, t):
@@ -186,13 +186,14 @@
     def spread(q, j, t, peer, slot):
         return remote(
             total.at[q, j, t, slot], total.at[q, j, t, slot],
-            gs_sem.at[q, j, t, peer], gr_sem.at[q, j, t, slot], {"band": z_band(peer)},
-        )
-
-    def to_mate(q, j, t, slot):
-        return remote(
-            total.at[q, j, t, slot], mate.at[q, j, t, slot],
-            ms_sem.at[q, j, t, slot], mr_sem.at[q, j, t, slot], {"band": mate_band},
+            gs_sem.at[q, j, t], gr_sem.at[q, j, t],
+            {"band": z_band(turn_z(1) if peer is others else peer)},
+        )
+
+    def to_mate(q, j, t):
+        return remote(
+            total.at[q, j, t], mate.at[q, j, t],
+            ms_sem.at[q, j, t], mr_sem.at[q, j, t], {"band": mate_band},
         )
 
     def sum_a(q, j, t):
@@ -211,8 +212,7 @@
         gathered[q, j, t, z] = part[q, j, t, z]
 
     def sum_c(q, j, t):
-        for o in FAR:
-            scatter(q, j, t, turn_z(o), turn_z(o)).wait_recv()
+        scatter(q, j, t, others, others).wait_recv()
         value = gathered[q, j, t, 0]
         for k in range(1, NZ):
             value = value + gathered[q, j, t, k]
@@ -224,16 +224,13 @@
         total[q, j, t, z] = summed[q, j, t] + other[q, j, t]
         for o in FAR:
             spread(q, j, t, turn_z(o), z).start()
-        to_mate(q, j, t, z).start()
 
     def sum_e(q, j, t):
-        for o in NEAR:
-            spread(q, j, t, turn_z(o), turn_z(o)).wait_recv()
-            to_mate(q, j, t, turn_z(o)).start()
+        spread(q, j, t, others, others).wait_recv()
+        to_mate(q, j, t).start()
 
     def sum_f(q, j, t):
-        for o in (0,) + NEAR:
-            to_mate(q, j, t, turn_z(o)).wait_recv()
+        to_mate(q, j, t).wait_recv()
 
         def step(k, _):
             full[q, j, t, k, pl.ds(4 * core, PART)] = total[q, j, t, k]
@@ -264,13 +261,18 @@
     for fetch in fetches[1:]:
         fetch.wait()
 
-    low = me * NX + lane_y[...]
-    low = jnp.where(low <= NG // 2, low, low - NG)
-    flat = low * low + lane_z[...]
+    def square(value):
+        value = jnp.where(value <= NG // 2, value, value - NG)
+        return value * value
+
+    lane = lax.broadcasted_iota(jnp.int32, (8, CHUNK), 1)
+    lane_y = (lane * 683) >> 16
+    flat = square(me * NX + lane_y) + square(lane - NG * lane_y)
+    row = lax.broadcasted_iota(jnp.int32, (8, CHUNK), 0)
 
     def coulomb_rows(k, _):
         rows = pl.ds(pl.multiple_of(8 * k, 8), 8)
-        squared = jnp.concatenate([row_x[rows, :]] * 9, axis=1) + flat
+        squared = square(8 * k + row) + flat
         weight = mask_ref[rows, :].astype(F32)
         scale = -EXCHANGE_MIX * COULOMB / float(NG**3)
         coulomb[rows, :] = scale * weight / jnp.maximum(squared, 1).astype(F32)
@@ -305,13 +307,13 @@
 
     def transform_y(p0, p1):
         vh, vl = split(jnp.concatenate([p0, p1], axis=1))
-        out = dot(left_y[...], jnp.concatenate([vh, vl], axis=0))
+        out = dot(weights[:192, :192], jnp.concatenate([vh, vl], axis=0))
         out = out[:NG] + out[NG:]
         return out[:, :128], out[:, 128:]
 
     def transform_z(value):
         vh, vl = split(value)
-        out = dot(jnp.concatenate([vh, vl], axis=1), right_z[...])
+        out = dot(jnp.concatenate([vh, vl], axis=1), weights[192:448, :])
         return out[:, :128] + out[:, 128:]
 
     def forward(j, t):
@@ -344,16 +346,15 @@
 
     def middle(j):
         for t in range(NT):
-            for o in range(1, NF):
-                copy_a(j, t, turn(o), turn(o)).wait_recv()
+            copy_a(j, t, others, others).wait_recv()
 
         def step(s, _):
             cols = pl.ds(pl.multiple_of(384 * s, 128), 384)
             value = recv_a[j, :, :, :, cols].reshape(NL * NG, 384)
-            spectrum = left_product(left_fx[...], value)
+            spectrum = left_product(weights[448:832, :192], value)
             weight = coulomb[:, cols]
             scaled = jnp.concatenate([spectrum[:NG] * weight, spectrum[NG:] * weight], axis=0)
-            back = left_product(left_bx[...], scaled)
+            back = left_product(weights[832:1216, :192], scaled)
             send_b[j, :, :, :, cols] = back.reshape(NT, NF, 8, 384)
             return 0
 
@@ -364,8 +365,7 @@
             recv_b[j, t, me] = send_b[j, t, me]
 
     def backward(j, t):
-        for o in range(1, NF):
-            copy_b(j, t, turn(o), turn(o)).wait_recv()
+        copy_b(j, t, others, others).wait_recv()
 
         def half(h, _):
             planes = []
@@ -426,13 +426,11 @@
         lax.fori_loop(0, LANES // 128, step, 0, unroll=4)
 
     def receive(j, t):
-        sum_e(0, j, t)
         sum_f(0, j, t)
         open_blk(j, t)
         forward(j, t)
 
     def finish(j, t):
-        sum_e(1, j, t)
         sum_f(1, j, t)
         write_block(j, t)
 
@@ -450,18 +448,35 @@
     sum_d(0, 0, 1)
     sum_b(0, 1, 2)
     sum_d(0, 0, 2)
+    sum_e(0, 0, 0)
     sum_d(0, 1, 0)
     receive(0, 0)
     sum_c(0, 1, 1)
+    sum_e(0, 0, 1)
+    sum_c(0, 1, 2)
     receive(0, 1)
     sum_d(0, 1, 1)
-    sum_c(0, 1, 2)
+    sum_e(0, 0, 2)
+    sum_d(0, 1, 2)
     receive(0, 2)
-    sum_d(0, 1, 2)
+    sum_e(0, 1, 0)
     receive(1, 0)
+    sum_e(0, 1, 1)
     receive(1, 1)
+    sum_e(0, 1, 2)
     receive(1, 2)
+
+    def sum_sent(q, j, t):
+        to_pair(q, j, t).wait_send()
+        to_y(q, j, t).wait_send()
+        to_mate(q, j, t).wait_send()
+        scatter(q, j, t, others, others).wait_send()
+        spread(q, j, t, others, others).wait_send()
+
     middle(0)
+    for j in range(NL):
+        for t in range(NT):
+            sum_sent(0, j, t)
     middle(1)
 
     def back(j, t):
@@ -470,51 +485,51 @@
         sum_a(1, j, t)
 
     back(0, 0)
+    back(0, 1)
     sum_b(1, 0, 0)
-    back(0, 1)
+    back(0, 2)
     sum_b(1, 0, 1)
-    back(0, 2)
+    back(1, 0)
     sum_b(1, 0, 2)
     sum_c(1, 0, 0)
-    back(1, 0)
+    back(1, 1)
     sum_b(1, 1, 0)
     sum_c(1, 0, 1)
-    sum_d(1, 0, 0)
-    back(1, 1)
+    back(1, 2)
     sum_b(1, 1, 1)
     sum_c(1, 0, 2)
+    sum_d(1, 0, 0)
+    lax.fori_loop(0, QUADS // 2, write_local, 0, unroll=2)
+    sum_b(1, 1, 2)
+    lax.fori_loop(QUADS // 2, QUADS, write_local, 0, unroll=2)
+    local_out = pltpu.make_async_copy(local_ref, local_hbm, out_sem.at[NT])
+    local_out.start()
     sum_d(1, 0, 1)
-    back(1, 2)
     sum_c(1, 1, 0)
     sum_d(1, 0, 2)
-    sum_b(1, 1, 2)
-    lax.fori_loop(0, QUADS, write_local, 0, unroll=2)
-    local_out = pltpu.make_async_copy(local_ref, local_hbm, out_sem.at[NT])
-    local_out.start()
     sum_c(1, 1, 1)
     sum_d(1, 1, 0)
-    finish(0, 0)
+    sum_c(1, 1, 2)
     sum_d(1, 1, 1)
-    finish(0, 1)
-    sum_c(1, 1, 2)
-    finish(0, 2)
     sum_d(1, 1, 2)
     for t in range(NT):
-        finish(1, t)
-        block_out(t).start()
+        sum_e(1, 0, t)
     for t in range(NT):
-        for j in range(NL):
-            for o in range(1, NF):
-                copy_a(j, t, turn(o), me).wait_send()
-                copy_b(j, t, turn(o), me).wait_send()
-            for q in range(2):
-                to_pair(q, j, t).wait_send()
-                to_y(q, j, t).wait_send()
-                to_mate(q, j, t, z).wait_send()
-                for o in range(1, NZ):
-                    scatter(q, j, t, turn_z(o), z).wait_send()
-                    spread(q, j, t, turn_z(o), z).wait_send()
-                    to_mate(q, j, t, turn_z(o)).wait_send()
+        finish(0, t)
+    for j in range(NL):
+        for t in range(NT):
+            copy_a(j, t, others, others).wait_send()
+            copy_b(j, t, others, others).wait_send()
+    for t in range(NT):
+        sum_e(1, 1, t)
+        if t > 0:
+            finish(1, t - 1)
+            block_out(t - 1).start()
+    finish(1, NT - 1)
+    block_out(NT - 1).start()
+    for j in range(NL):
+        for t in range(NT):
+            sum_sent(1, j, t)
     local_out.wait()
     for t in range(NT):
         block_out(t).wait()
@@ -534,31 +549,31 @@
     pieces = buffer(2, NL, NT, NZ, PART, 4, 128)
     single = buffer(2, NL, NT, PART, 4, 128)
     grid = buffer(NL, NT, NF, 8, CHUNK)
-    constants = [jnp.asarray(t) for t in tables()]
+    constants = jnp.asarray(tables())
     flat = jax.ShapeDtypeStruct((NX, NL, LANES), F32)
-    many = dma((NL, NT, NF))
-    bulk = dma((2, NL, NT, NZ))
+    many = dma((NL, NT))
     few = dma((2, NL, NT))
     anywhere = pl.BlockSpec(memory_space=pl.ANY)
+    stay = pl.BlockSpec(memory_space=pltpu.HBM)
     orb = orbitals.transpose(1, 0, 2)
     local, block = pl.pallas_call(
         kernel,
         out_shape=(flat, flat),
-        in_specs=[anywhere, pl.BlockSpec(memory_space=pltpu.SMEM)]
-        + [anywhere] * (1 + len(constants)),
+        in_specs=[stay, pl.BlockSpec(memory_space=pltpu.SMEM)]
+        + [stay] * 2,
         out_specs=(anywhere, anywhere),
         scratch_shapes=[
-            like(orb), like(cutoff_mask), *[like(c) for c in constants],
-            like(flat), like(flat), dma((2 + len(constants),)), dma((NT + 1,)),
+            like(orb), like(cutoff_mask), like(constants),
+            like(flat), like(flat), dma((3,)), dma((NT + 1,)),
             buffer(NG, CHUNK), tiles, tiles, planes, planes,
             buffer(PLANES, 128), planes, planes, grid, grid, grid, grid,
             pieces, pieces, pieces, single, single, pieces, pieces,
-            many, many, many, many, few, few, few, few, bulk, bulk, bulk, bulk, bulk, bulk,
+            many, many, many, many, few, few, few, few, few, few, few, few, few, few,
         ],
         compiler_params=pltpu.CompilerParams(
             collective_id=0, has_side_effects=True, vmem_limit_bytes=60 << 20
         ),
-    )(orb, owners, cutoff_mask, *constants)
+    )(orb, owners, cutoff_mask, constants)
     return local.transpose(1, 0, 2), block.transpose(1, 0, 2)
 
 

time: 107 us -> 97.3 us (0.909)
  Pallas kernels: 102 us -> 92.7 us
    pallas_call x1, Pallas kernels: 102 us -> 92.7 us  [per_device(): pl.pallas_call(kernel, out_shape=(flat, flat), in_specs=[stay, pl.BlockSp...]
where the time goes in v5:
time: 97.3 us; the launch traced here: 97.1 us
  Pallas kernels  92.7 us (95%)
  local copies, waits for them, and re-layouts  3.13 us (3%)
  between operations  1.29 us (1%)
    pallas_call x1, Pallas kernels, per_device(): pl.pallas_call(kernel, out_shape=(flat, flat), in_specs=[stay, pl.BlockSp...  92.7 us
    unnamed x4, local copies, waits for them, and re-layouts  3.13 us

profile of v5, /device:TPU:1, one launch (start us, length us, event | category | flops | bytes accessed | tf_op | source)
XLA Modules:
  0.0 97.1 jit_solution(13161934561414676896)
XLA Ops:
  1.3 92.7 %shard_map.59 = (f32[12,2,9216]{2,1,0:T(2,128)}, f32[12,2,9216]{2,1,0:T(2,128)}) custom-call(f32[12,2,9216]{2,1,0:T(2,128)} %bitcast.3, s32[1]{0:T(128)S(6)} %copy.8.owner_ref, s32[96,1152]{1,0:T(8,128)} %mask_hbm.1, bf16[1216,256]{1,0:T(8,128)(2,1)} %constant.2.clone.weights_hbm), custom_call_target="tpu_custom_call" | custom-call | tf_op jit(solution)/shard_map/pallas_call | solution.py:559
  94.0 0.0 copy-start
  94.0 2.2 %copy.9 = f32[2,12,9216]{2,0,1:T(2,128)} copy(f32[2,12,9216]{2,0,1:T(2,128)} %bitcast.5) | data formatting | bytes 1769472
  96.2 0.0 copy-done
  96.2 0.9 copy.10
Async XLA Ops:
  94.0 2.2 %copy-start = (f32[12,2,9216]{2,1,0:T(2,128)S(1)}, f32[12,2,9216]{2,1,0:T(2,128)}, u32[]{:S(2)}) copy-start(f32[12,2,9216]{2,1,0:T(2,128)} %get-tuple-element.5) | copy-start | bytes 2654212

commit v6 on v5

--- a/solution.py
+++ b/solution.py
@@ -129,12 +129,14 @@
     def turn_z(o):
         return lax.rem(z + o, NZ)
 
-    inputs = (
-        (orb_hbm, orb_ref), (mask_hbm, mask_ref), (weights_hbm, weights),
-    )
-    fetches = [
-        pltpu.make_async_copy(src, dst, in_sem.at[n]) for n, (src, dst) in enumerate(inputs)
-    ]
+    fetches = []
+    for t in range(NT):
+        rows = pl.ds(4 * t, 4)
+        fetches.append(
+            pltpu.make_async_copy(orb_hbm.at[rows], orb_ref.at[rows], in_sem.at[t])
+        )
+    fetches.append(pltpu.make_async_copy(mask_hbm, mask_ref, in_sem.at[NT]))
+    fetches.append(pltpu.make_async_copy(weights_hbm, weights, in_sem.at[NT + 1]))
     for fetch in fetches:
         fetch.start()
     barrier = pltpu.get_barrier_semaphore()
@@ -249,8 +251,9 @@
                 source[0, j, t, c // 9, c % 9] = jnp.where(mine, tile[:, j, :], 0.0)
         return 0
 
-    fetches[0].wait()
-    lax.fori_loop(0, LANES // 128, load_tiles, 0, unroll=4)
+    for fetch in fetches[:NT]:
+        fetch.wait()
+    lax.fori_loop(0, LANES // 128, load_tiles, 0, unroll=8)
     pl.semaphore_wait(barrier, len(devices))
     for j in range(NL):
         for t in range(NT):
@@ -258,7 +261,7 @@
     for t in range(NT):
         sum_b(0, 0, t)
     sum_b(0, 1, 0)
-    for fetch in fetches[1:]:
+    for fetch in fetches[NT:]:
         fetch.wait()
 
     def square(value):
@@ -303,7 +306,7 @@
                 blk_u[t, half_plane(4 * a + b, j), :] = quad[b]
             return 0
 
-        lax.fori_loop(0, QUADS, step, 0, unroll=4)
+        lax.fori_loop(0, QUADS, step, 0, unroll=8)
 
     def transform_y(p0, p1):
         vh, vl = split(jnp.concatenate([p0, p1], axis=1))
@@ -326,7 +329,7 @@
             turned[across(2 * s + 1), :] = out1
             return 0
 
-        lax.fori_loop(0, 4, rows, 0, unroll=2)
+        lax.fori_loop(0, 4, rows, 0, unroll=4)
 
         def half(h, _):
             out = transform_z(turned[pl.ds(pl.multiple_of(384 * h, 8), 384), :])
@@ -398,7 +401,7 @@
             )
             return 0
 
-        lax.fori_loop(0, 4, rows, 0, unroll=2)
+        lax.fori_loop(0, 4, rows, 0, unroll=4)
 
     def close_block(j, t):
         def step(a, _):
@@ -407,7 +410,7 @@
                 source[1, j, t, a // 3, (a % 3) * 3 + k] = tiles[k]
             return 0
 
-        lax.fori_loop(0, QUADS, step, 0, unroll=4)
+        lax.fori_loop(0, QUADS, step, 0, unroll=8)
 
     def write_local(a, _):
         for t in range(NT):
@@ -417,13 +420,14 @@
                 local_ref[4 * t : 4 * t + 4, :, lanes] = tiles[k].reshape(4, NL, 128)
         return 0
 
-    def write_block(j, t):
-        def step(c, _):
-            lanes = pl.ds(pl.multiple_of(c * 128, 128), 128)
-            block_ref[4 * t : 4 * t + 4, j, lanes] = full[1, j, t, c // 9, c % 9]
-            return 0
-
-        lax.fori_loop(0, LANES // 128, step, 0, unroll=4)
+    def write_half(j, t, piece, first):
+        def step(k, _):
+            for n in range(PART):
+                lanes = pl.ds(pl.multiple_of((9 * k + first + n) * 128, 128), 128)
+                block_ref[4 * t : 4 * t + 4, j, lanes] = piece[1, j, t, k, n]
+            return 0
+
+        lax.fori_loop(0, NZ, step, 0, unroll=2)
 
     def receive(j, t):
         sum_f(0, j, t)
@@ -431,8 +435,9 @@
         forward(j, t)
 
     def finish(j, t):
-        sum_f(1, j, t)
-        write_block(j, t)
+        write_half(j, t, total, 4 * core)
+        to_mate(1, j, t).wait_recv()
+        write_half(j, t, mate, 4 * (1 - core))
 
     def block_out(t):
         return pltpu.make_async_copy(
@@ -564,7 +569,7 @@
         out_specs=(anywhere, anywhere),
         scratch_shapes=[
             like(orb), like(cutoff_mask), like(constants),
-            like(flat), like(flat), dma((3,)), dma((NT + 1,)),
+            like(flat), like(flat), dma((NT + 2,)), dma((NT + 1,)),
             buffer(NG, CHUNK), tiles, tiles, planes, planes,
             buffer(PLANES, 128), planes, planes, grid, grid, grid, grid,
             pieces, pieces, pieces, single, single, pieces, pieces,

time: 97.3 us -> 95.7 us (0.984)
  Pallas kernels: 92.7 us -> 91.1 us
    pallas_call x1, Pallas kernels: 92.7 us -> 91.1 us  [per_device(): pl.pallas_call(kernel, out_shape=(flat, flat), in_specs=[stay, pl.BlockSp...]
where the time goes in v6:
time: 95.7 us; the launch traced here: 95.6 us
  Pallas kernels  91.1 us (95%)
  local copies, waits for them, and re-layouts  3.13 us (3%)
  between operations  1.29 us (1%)
    pallas_call x1, Pallas kernels, per_device(): pl.pallas_call(kernel, out_shape=(flat, flat), in_specs=[stay, pl.BlockSp...  91.1 us
    unnamed x4, local copies, waits for them, and re-layouts  3.13 us

profile of v6, /device:TPU:1, one launch (start us, length us, event | category | flops | bytes accessed | tf_op | source)
XLA Modules:
  0.0 95.6 jit_solution(4551150038054371467)
XLA Ops:
  1.3 91.1 %shard_map.59 = (f32[12,2,9216]{2,1,0:T(2,128)}, f32[12,2,9216]{2,1,0:T(2,128)}) custom-call(f32[12,2,9216]{2,1,0:T(2,128)} %bitcast.3, s32[1]{0:T(128)S(6)} %copy.8.owner_ref, s32[96,1152]{1,0:T(8,128)} %mask_hbm.1, bf16[1216,256]{1,0:T(8,128)(2,1)} %constant.2.clone.weights_hbm), custom_call_target="tpu_custom_call" | custom-call | tf_op jit(solution)/shard_map/pallas_call | solution.py:564
  92.4 0.0 copy-start
  92.4 2.2 %copy.9 = f32[2,12,9216]{2,0,1:T(2,128)} copy(f32[2,12,9216]{2,0,1:T(2,128)} %bitcast.5) | data formatting | bytes 1769472
  94.7 0.0 copy-done
  94.7 0.9 copy.10
Async XLA Ops:
  92.4 2.2 %copy-start = (f32[12,2,9216]{2,1,0:T(2,128)S(1)}, f32[12,2,9216]{2,1,0:T(2,128)}, u32[]{:S(2)}) copy-start(f32[12,2,9216]{2,1,0:T(2,128)} %get-tuple-element.5) | copy-start | bytes 2654212

commit v7 on v6

--- a/solution.py
+++ b/solution.py
@@ -490,28 +490,28 @@
         sum_a(1, j, t)
 
     back(0, 0)
+    sum_b(1, 0, 0)
     back(0, 1)
-    sum_b(1, 0, 0)
+    sum_b(1, 0, 1)
     back(0, 2)
-    sum_b(1, 0, 1)
-    back(1, 0)
     sum_b(1, 0, 2)
     sum_c(1, 0, 0)
-    back(1, 1)
+    back(1, 0)
     sum_b(1, 1, 0)
     sum_c(1, 0, 1)
-    back(1, 2)
+    back(1, 1)
     sum_b(1, 1, 1)
     sum_c(1, 0, 2)
     sum_d(1, 0, 0)
+    back(1, 2)
     lax.fori_loop(0, QUADS // 2, write_local, 0, unroll=2)
     sum_b(1, 1, 2)
+    sum_d(1, 0, 1)
+    sum_c(1, 1, 0)
+    sum_d(1, 0, 2)
     lax.fori_loop(QUADS // 2, QUADS, write_local, 0, unroll=2)
     local_out = pltpu.make_async_copy(local_ref, local_hbm, out_sem.at[NT])
     local_out.start()
-    sum_d(1, 0, 1)
-    sum_c(1, 1, 0)
-    sum_d(1, 0, 2)
     sum_c(1, 1, 1)
     sum_d(1, 1, 0)
     sum_c(1, 1, 2)

time: 95.7 us -> 93.6 us (0.978)
  Pallas kernels: 91.1 us -> 89 us
    pallas_call x1, Pallas kernels: 91.1 us -> 89 us  [per_device(): pl.pallas_call(kernel, out_shape=(flat, flat), in_specs=[stay, pl.BlockSp...]
where the time goes in v7:
time: 93.6 us; the launch traced here: 93.5 us
  Pallas kernels  89 us (95%)
  local copies, waits for them, and re-layouts  3.13 us (3%)
  between operations  1.29 us (1%)
    pallas_call x1, Pallas kernels, per_device(): pl.pallas_call(kernel, out_shape=(flat, flat), in_specs=[stay, pl.BlockSp...  89 us
    unnamed x4, local copies, waits for them, and re-layouts  3.13 us

profile of v7, /device:TPU:1, one launch (start us, length us, event | category | flops | bytes accessed | tf_op | source)
XLA Modules:
  0.0 93.5 jit_solution(13612344964656199864)
XLA Ops:
  1.3 89.0 %shard_map.59 = (f32[12,2,9216]{2,1,0:T(2,128)}, f32[12,2,9216]{2,1,0:T(2,128)}) custom-call(f32[12,2,9216]{2,1,0:T(2,128)} %bitcast.3, s32[1]{0:T(128)S(6)} %copy.8.owner_ref, s32[96,1152]{1,0:T(8,128)} %mask_hbm.1, bf16[1216,256]{1,0:T(8,128)(2,1)} %constant.2.clone.weights_hbm), custom_call_target="tpu_custom_call" | custom-call | tf_op jit(solution)/shard_map/pallas_call | solution.py:564
  90.3 0.0 copy-start
  90.3 2.2 %copy.9 = f32[2,12,9216]{2,0,1:T(2,128)} copy(f32[2,12,9216]{2,0,1:T(2,128)} %bitcast.5) | data formatting | bytes 1769472
  92.5 0.0 copy-done
  92.5 0.9 copy.10
Async XLA Ops:
  90.3 2.2 %copy-start = (f32[12,2,9216]{2,1,0:T(2,128)S(1)}, f32[12,2,9216]{2,1,0:T(2,128)}, u32[]{:S(2)}) copy-start(f32[12,2,9216]{2,1,0:T(2,128)} %get-tuple-element.5) | copy-start | bytes 2654212

commit v8 on v7

--- a/solution.py
+++ b/solution.py
@@ -446,12 +446,12 @@
 
     sum_c(0, 0, 0)
     sum_c(0, 0, 1)
+    sum_b(0, 1, 1)
     sum_c(0, 0, 2)
     sum_d(0, 0, 0)
-    sum_b(0, 1, 1)
+    sum_b(0, 1, 2)
     sum_c(0, 1, 0)
     sum_d(0, 0, 1)
-    sum_b(0, 1, 2)
     sum_d(0, 0, 2)
     sum_e(0, 0, 0)
     sum_d(0, 1, 0)
@@ -460,10 +460,10 @@
     sum_e(0, 0, 1)
     sum_c(0, 1, 2)
     receive(0, 1)
+    sum_e(0, 0, 2)
+    receive(0, 2)
     sum_d(0, 1, 1)
-    sum_e(0, 0, 2)
     sum_d(0, 1, 2)
-    receive(0, 2)
     sum_e(0, 1, 0)
     receive(1, 0)
     sum_e(0, 1, 1)

time: 93.6 us -> 92.5 us (0.988)
  Pallas kernels: 89 us -> 88 us
    pallas_call x1, Pallas kernels: 89 us -> 88 us  [per_device(): pl.pallas_call(kernel, out_shape=(flat, flat), in_specs=[stay, pl.BlockSp...]
where the time goes in v8:
time: 92.5 us; the launch traced here: 92.4 us
  Pallas kernels  88 us (95%)
  local copies, waits for them, and re-layouts  3.13 us (3%)
  between operations  1.29 us (1%)
    pallas_call x1, Pallas kernels, per_device(): pl.pallas_call(kernel, out_shape=(flat, flat), in_specs=[stay, pl.BlockSp...  88 us
    unnamed x4, local copies, waits for them, and re-layouts  3.13 us

profile of v8, /device:TPU:1, one launch (start us, length us, event | category | flops | bytes accessed | tf_op | source)
XLA Modules:
  0.0 92.4 jit_solution(9003681630318908472)
XLA Ops:
  1.3 88.0 %shard_map.59 = (f32[12,2,9216]{2,1,0:T(2,128)}, f32[12,2,9216]{2,1,0:T(2,128)}) custom-call(f32[12,2,9216]{2,1,0:T(2,128)} %bitcast.3, s32[1]{0:T(128)S(6)} %copy.8.owner_ref, s32[96,1152]{1,0:T(8,128)} %mask_hbm.1, bf16[1216,256]{1,0:T(8,128)(2,1)} %constant.2.clone.weights_hbm), custom_call_target="tpu_custom_call" | custom-call | tf_op jit(solution)/shard_map/pallas_call | solution.py:564
  89.2 0.0 copy-start
  89.2 2.2 %copy.9 = f32[2,12,9216]{2,0,1:T(2,128)} copy(f32[2,12,9216]{2,0,1:T(2,128)} %bitcast.5) | data formatting | bytes 1769472
  91.5 0.0 copy-done
  91.5 0.9 copy.10
Async XLA Ops:
  89.2 2.2 %copy-start = (f32[12,2,9216]{2,1,0:T(2,128)S(1)}, f32[12,2,9216]{2,1,0:T(2,128)}, u32[]{:S(2)}) copy-start(f32[12,2,9216]{2,1,0:T(2,128)} %get-tuple-element.5) | copy-start | bytes 2654212
